TPU v7x, 256 devices: a whole 4x4x8 slice. The times are simulated.
256 devices in a mesh: mem: 64 (over z, x_lo, y), band: 4 (over x_hi, core).
Axes of the slice: x: 4 (x_hi: 2, x_lo: 2; x = x_hi * 2 + x_lo), y: 4, z: 8, core: 2. Of those that a mesh axis runs over, the one named last changes fastest.
Arguments:
- alpha: bfloat16 [128, 4, 320, 720], P('mem', None, 'band'), may hold values from -6 to 6
- static_ctl: bfloat16 [4, 320, 720], P(None, 'band'), may hold values from -6 to 6
- perturbations: bfloat16 [128, 4, 320, 720], P('mem', None, None, 'band'), may hold values from -16 to 16
- static_std: float32 [4, 320, 720], P(None, None, 'band'), may hold values from 0.5 to 2
- lon_root: bfloat16 [720, 720], replicated, may hold values from -0.11 to 1.11
- lat_root: bfloat16 [320, 320], replicated, may hold values from -0.11 to 1.11
- jacobian: bfloat16 [32, 4, 320, 720], P(None, None, 'mem', 'band'), may hold values from -3 to 3
- obs_count: int32 [320, 720], P('mem', 'band'), may hold values from 1 to 6
- channel_mask: int32 [32, 320, 720], P(None, 'mem', 'band'), may hold values 0 or 1
- channel_error: float32 [32], replicated, may hold values from 1 to 2
- member_weight: int32 [128], replicated, may hold values from 1 to 4
Outputs:
- grad_alpha: float32 [128, 4, 320, 720], P('mem', None, 'band')
- grad_static: float32 [4, 320, 720], P(None, 'band')
All inputs are finite; a program needn't handle non-finite values. No bound on the sum of `channel_mask` on one device may be relied on, other than what follows from the above.
Results may differ from a plain program's by a relative error of at most 0.0055.
Values may be sent and summed in bfloat16 or wider, within the bound.
A program may use at most 64 MiB of HBM per device.

v0:
```python
import jax
import jax.numpy as jnp
from jax import lax
from jax.sharding import PartitionSpec as P


def in_blocks(x, dim, devices):
    lengths = x.shape
    pieces = x.reshape(*lengths[:dim], devices, lengths[dim] // devices, *lengths[dim + 1 :])
    return jnp.moveaxis(pieces, dim, 0)


def sum_at_owner(x, axis, dim):
    pieces = in_blocks(x, dim, lax.axis_size(axis))
    arrived = lax.all_to_all(pieces, axis, split_axis=0, concat_axis=0, tiled=True)
    return arrived.sum(axis=0)


def laid_out(pieces, dim):
    lengths = list(pieces.shape[1:])
    lengths[dim] *= pieces.shape[0]
    return jnp.moveaxis(pieces, 0, dim).reshape(lengths)


def from_everyone(x, axis):
    devices = lax.axis_size(axis)
    return lax.all_to_all(jnp.broadcast_to(x[None], (devices, *x.shape)), axis, 0, 0, tiled=True)


def collect(x, axis, dim):
    return laid_out(from_everyone(x, axis), dim)


def shards(
    alpha,
    static_ctl,
    perturbations,
    static_std,
    lon_root,
    lat_root,
    jacobian,
    obs_count,
    channel_mask,
    channel_error,
    member_weight,
):
    members = alpha.shape[0]
    rows = jacobian.shape[2]
    rank = lax.axis_index("mem")
    weights = member_weight.astype(jnp.float32)
    coef = weights / jnp.sqrt(jnp.sum(weights * weights))
    own_coef = lax.dynamic_slice_in_dim(coef, rank * members, members, 0)
    fields = jnp.concatenate([alpha, static_ctl[None]], axis=0)
    along_lon = jnp.dot(fields, lon_root, preferred_element_type=jnp.float32).astype(jnp.bfloat16)
    regrouped = lax.all_to_all(along_lon, "band", split_axis=3, concat_axis=2, tiled=True)
    along_lat = jnp.einsum("ij,msjk->msik", lat_root, regrouped, preferred_element_type=jnp.float32)
    member_lat = along_lat[:members]
    own_static = lax.dynamic_slice_in_dim(along_lat[members], rank * rows, rows, 1)
    scaled = 0.8 * own_coef
    ensemble_term = jnp.sum(
        scaled[:, None, None, None] * perturbations.astype(jnp.float32) * member_lat, axis=0
    )
    own_sum = sum_at_owner(ensemble_term, "mem", 1)
    own_std = lax.dynamic_slice_in_dim(static_std, rank * rows, rows, 1)
    increment = own_sum + 0.6 * own_std * own_static
    obs_weight = (
        channel_mask.astype(jnp.float32)
        * obs_count.astype(jnp.float32)[None]
        / (channel_error * channel_error)[:, None, None]
    )
    jac_full = jacobian.astype(jnp.float32)
    radiance = jnp.sum(jac_full * increment[None], axis=1)
    obs_gradient = jnp.sum(jac_full * (obs_weight * radiance)[:, None], axis=0).astype(jnp.bfloat16)
    band_gradient = collect(obs_gradient, "mem", 1).astype(jnp.float32)
    member_adjoint = (
        scaled[:, None, None, None] * perturbations.astype(jnp.float32) * band_gradient[None]
    ).astype(jnp.bfloat16)
    static_adjoint = (0.6 * static_std * band_gradient).astype(jnp.bfloat16)
    adjoints = jnp.concatenate([member_adjoint, static_adjoint[None]], axis=0)
    back_lat = jnp.einsum(
        "ji,msjk->msik", lat_root, adjoints, preferred_element_type=jnp.float32
    ).astype(jnp.bfloat16)
    returned = lax.all_to_all(back_lat, "band", split_axis=2, concat_axis=3, tiled=True)
    back_lon = jnp.einsum("msil,jl->msij", returned, lon_root, preferred_element_type=jnp.float32)
    grad_alpha = alpha.astype(jnp.float32) + back_lon[:members]
    grad_static = static_ctl.astype(jnp.float32) + back_lon[members]
    return (grad_alpha, grad_static)


def solution(mesh):
    in_specs = (
        P("mem", None, "band", None),
        P(None, "band", None),
        P("mem", None, None, "band"),
        P(None, None, "band"),
        P(),
        P(),
        P(None, None, "mem", "band"),
        P("mem", "band"),
        P(None, "mem", "band"),
        P(),
        P(),
    )
    out_specs = (P("mem", None, "band", None), P(None, "band", None))
    return jax.shard_map(shards, mesh=mesh, in_specs=in_specs, out_specs=out_specs, check_vma=False)
```

profile of v0, /device:TPU:1, one launch (start us, length us, event | category | flops | bytes accessed | tf_op | source)
XLA Modules:
  0.0 176.1 jit_solution(13423768554717504345)
XLA Ops:
  0.6 1.2 copy-done
  1.9 2.7 %convolution_convert_fusion.1 = bf16[3,4,80,720]{3,2,1,0:T(8,128)(2,1)S(1)} fusion(bf16[1,4,80,720]{3,2,1,0:T(8,128)(2,1)} %bitcast.49, bf16[2,4,80,720]{3,2,1,0:T(8,128)(2,1)} %param.11, bf16[720,720]{1,0:T(8,128)(2,1)S(1)} %copy-done), kind=kOutput, calls=%fused_computation.10 | convolution fusion | flops 996710400 | bytes 3801600 | tf_op jit(solution)/shard_map/dot_general | solution.py:54
  4.6 3.2 %copy.32 = bf16[3,4,80,720]{2,1,0,3:T(4,128)(2,1)} copy(bf16[3,4,80,720]{3,2,1,0:T(8,128)(2,1)S(1)} %convolution_convert_fusion.1) | data formatting | bytes 2764800 | tf_op jit(solution)/shard_map/convert_element_type | solution.py:54
  7.8 7.0 %all-to-all-start = ((bf16[3,4,80,720]{2,1,0,3:T(4,128)(2,1)}), bf16[3,4,80,720]{2,1,0,3:T(4,128)(2,1)S(1)}, u32[]{:S(2)}, u32[]{:S(2)}) async-start(bf16[3,4,80,720]{2,1,0,3:T(4,128)(2,1)} %copy.32), calls=%async_computation | async-start | bytes 4423680 | tf_op jit(solution)/shard_map/all_to_all | solution.py:55
  16.2 26.2 %all-to-all-done = bf16[3,4,80,720]{2,1,0,3:T(4,128)(2,1)S(1)} async-done(((bf16[3,4,80,720]{2,1,0,3:T(4,128)(2,1)}), bf16[3,4,80,720]{2,1,0,3:T(4,128)(2,1)S(1)}, u32[]{:S(2)}, u32[]{:S(2)}) %all-to-all-start) | async-done | bytes 1382432 | tf_op jit(solution)/shard_map/all_to_all | solution.py:55
  42.3 3.8 %copy.33 = bf16[3,4,80,4,180]{4,2,3,1,0:T(8,128)(2,1)} copy(bf16[3,4,80,4,180]{2,1,0,4,3:T(4,128)(2,1)S(1)} %bitcast.44) | data formatting | bytes 2764800 | tf_op jit(solution)/shard_map/all_to_all | solution.py:55
  46.1 3.3 %convolution_bitcast_fusion = f32[3,4,320,180]{2,3,1,0:T(8,128)S(1)} fusion(bf16[3,4,320,180]{3,2,1,0:T(8,128)(2,1)} %bitcast.46, bf16[320,320]{1,0:T(8,128)(2,1)} %param.16), kind=kOutput, calls=%fused_computation.5 | convolution fusion | flops 442368000 | bytes 4352000 | tf_op jit(solution)/shard_map/ij,msjk->msik/dot_general | solution.py:56
  49.4 1.7 copy-done.1
  51.5 1.5 copy.35
  53.0 11.1 %all-to-all-start.1 = ((f32[64,4,5,180]{3,1,2,0:T(4,128)}), f32[64,4,5,180]{3,1,2,0:T(4,128)S(1)}, u32[]{:S(2)}, u32[]{:S(2)}) async-start(f32[64,4,5,180]{3,1,2,0:T(4,128)} %bitcast.47), calls=%async_computation.1 | async-start | bytes 2621440 | tf_op jit(solution)/shard_map/all_to_all | solution.py:15
  64.7 2.1 %constant_dynamic-slice_fusion.1 = f32[4,5,180]{1,0,2:T(4,128)} fusion(f32[4,320,180]{1,0,2:T(4,128)} %param.14, s32[]{:T(128)S(6)} %select_n.8), kind=kLoop, calls=%fused_computation.38 | loop fusion | bytes 28804 | tf_op jit(solution)/shard_map/dynamic_slice | solution.py:64
  66.8 1.9 %copy.47 = f32[4,5,180]{2,0,1:T(4,128)} copy(f32[4,5,180]{1,0,2:T(4,128)} %constant_dynamic-slice_fusion.1) | data formatting | bytes 28800
  69.6 1.2 copy.37
  70.8 24.6 %all-to-all-done.1 = f32[64,4,5,180]{3,1,2,0:T(4,128)S(1)} async-done(((f32[64,4,5,180]{3,1,2,0:T(4,128)}), f32[64,4,5,180]{3,1,2,0:T(4,128)S(1)}, u32[]{:S(2)}, u32[]{:S(2)}) %all-to-all-start.1) | async-done | bytes 921632 | tf_op jit(solution)/shard_map/all_to_all | solution.py:15
  96.7 24.1 %all_to_all.46 = bf16[64,4,5,180]{3,1,2,0:T(4,128)(2,1)S(1)} all-to-all(bf16[64,4,5,180]{3,1,2,0:T(4,128)(2,1)S(1)} %broadcast_in_dim.7), channel_id=1, replica_groups=mesh['mem'=64,'band'=4] {'mem'}, dimensions={0} | all-to-all | bytes 921600 | tf_op jit(solution)/shard_map/all_to_all | solution.py:27
  121.9 1.5 fusion.18
  124.4 2.5 %fusion.4 = bf16[3,4,320,180]{2,3,1,0:T(8,128)(2,1)} fusion(bf16[1,4,320,180]{2,3,1,0:T(8,128)(2,1)S(1)} %fusion.18, bf16[2,4,320,180]{2,3,1,0:T(8,128)(2,1)S(1)} %multiply_convert_fusion, bf16[320,320]{1,0:T(8,128)(2,1)S(1)} %copy-done.7), kind=kOutput, calls=%fused_computation.11 | convolution fusion | flops 443750400 | bytes 2969600 | tf_op jit(solution)/shard_map/ji,msjk->msik/dot_general | solution.py:80
  127.0 6.7 %copy.41 = bf16[3,4,320,180]{3,1,0,2:T(4,128)(2,1)S(1)} copy(bf16[3,4,320,180]{2,3,1,0:T(8,128)(2,1)} %fusion.4) | data formatting | bytes 2764800 | tf_op jit(solution)/shard_map/convert_element_type | solution.py:82
  133.7 32.7 %all_to_all.47 = bf16[3,4,320,180]{3,1,0,2:T(4,128)(2,1)S(1)} all-to-all(bf16[3,4,320,180]{3,1,0,2:T(4,128)(2,1)S(1)} %copy.41), channel_id=1, replica_groups=mesh['mem'=64,'band'=4] {'band'}, dimensions={2} | all-to-all | bytes 2764800 | tf_op jit(solution)/shard_map/all_to_all | solution.py:83
  166.7 1.0 copy.43
  167.7 2.5 %all_to_all.41 = bf16[3,4,80,720]{3,2,1,0:T(8,128)(2,1)} reshape(bf16[3,4,80,4,180]{4,3,2,1,0:T(4,128)(2,1)S(1)} %copy.43) | data formatting | bytes 2764800 | tf_op jit(solution)/shard_map/all_to_all | solution.py:83
  170.2 2.8 %fusion.12 = f32[3,4,80,720]{3,2,1,0:T(8,128)S(1)} fusion(bf16[3,4,80,720]{3,2,1,0:T(8,128)(2,1)} %all_to_all.41, bf16[720,720]{1,0:T(8,128)(2,1)S(1)} %copy-done), kind=kOutput, calls=%fused_computation.18 | convolution fusion | flops 995328000 | bytes 5184000 | tf_op jit(solution)/shard_map/msil,jl->msij/dot_general | solution.py:84
  173.0 1.0 fusion.15
  174.6 1.5 slice_add_fusion
  (49 shorter events, 6.7 us)
Async XLA Ops:
  0.6 1.3 copy-start
  7.8 7.0 %copy-start.14 = (s32[128]{0:T(128)S(1)}, s32[128]{0:T(128)}, u32[]{:S(2)}) copy-start(s32[128]{0:T(128)} %param.21) | copy-start | bytes 1540
  7.8 34.5 %all-to-all-start = ((bf16[3,4,80,720]{2,1,0,3:T(4,128)(2,1)}), bf16[3,4,80,720]{2,1,0,3:T(4,128)(2,1)S(1)}, u32[]{:S(2)}, u32[]{:S(2)}) async-start(bf16[3,4,80,720]{2,1,0,3:T(4,128)(2,1)} %copy.32), calls=%async_computation | async-start | bytes 4423680 | tf_op jit(solution)/shard_map/all_to_all | solution.py:55
  16.1 33.2 %copy-start.11 = (f32[2]{0:T(128)}, f32[2]{0:T(128)S(1)}, u32[]{:S(2)}) copy-start(f32[2]{0:T(128)S(1)} %dynamic-slice_multiply_fusion) | copy-start | bytes 28
  46.1 5.0 %copy-start.2 = (bf16[2,4,320,180]{2,1,3,0:T(4,128)(2,1)S(1)}, bf16[2,4,320,180]{2,1,3,0:T(4,128)(2,1)}, u32[]{:S(2)}) copy-start(bf16[2,4,320,180]{2,1,3,0:T(4,128)(2,1)} %param.13) | copy-start | bytes 2764804
  49.4 1.7 copy-start.1
  53.0 11.2 %copy-start.15 = (f32[32]{0:T(128)S(1)}, f32[32]{0:T(128)}, u32[]{:S(2)}) copy-start(f32[32]{0:T(128)} %param.20) | copy-start | bytes 388
  53.0 11.7 %copy-start.10 = (s32[5,180]{1,0:T(8,128)S(1)}, s32[5,180]{1,0:T(8,128)}, u32[]{:S(2)}) copy-start(s32[5,180]{1,0:T(8,128)} %param.18) | copy-start | bytes 10804
  53.0 42.4 %all-to-all-start.1 = ((f32[64,4,5,180]{3,1,2,0:T(4,128)}), f32[64,4,5,180]{3,1,2,0:T(4,128)S(1)}, u32[]{:S(2)}, u32[]{:S(2)}) async-start(f32[64,4,5,180]{3,1,2,0:T(4,128)} %bitcast.47), calls=%async_computation.1 | async-start | bytes 2621440 | tf_op jit(solution)/shard_map/all_to_all | solution.py:15
  66.8 1.9 %slice-start = ((f32[3,4,320,180]{2,3,1,0:T(8,128)}), f32[1,4,320,180]{2,3,1,0:T(8,128)S(1)}, s32[]{:S(2)}) async-start(f32[3,4,320,180]{2,3,1,0:T(8,128)} %copy-done.1), calls=%async_computation.4 | async-start | bytes 2260992 | tf_op jit(solution)/shard_map/slice | solution.py:58
  69.6 26.1 %copy-start.9 = (f32[4,5,180]{2,0,1:T(4,128)S(1)}, f32[4,5,180]{2,0,1:T(4,128)}, u32[]{:S(2)}) copy-start(f32[4,5,180]{2,0,1:T(4,128)} %copy.47) | copy-start | bytes 43204
  69.6 26.1 %copy-start.4 = (bf16[32,4,5,180]{3,1,2,0:T(4,128)(2,1)S(1)}, bf16[32,4,5,180]{3,1,2,0:T(4,128)(2,1)}, u32[]{:S(2)}) copy-start(bf16[32,4,5,180]{3,1,2,0:T(4,128)(2,1)} %param.17) | copy-start | bytes 691204
  69.6 26.6 %copy-start.8 = (s32[32,5,180]{2,0,1:T(8,128)S(1)}, s32[32,5,180]{2,0,1:T(8,128)}, u32[]{:S(2)}) copy-start(s32[32,5,180]{2,0,1:T(8,128)} %param.19) | copy-start | bytes 345604
  69.6 26.6 %copy-start.13 = (f32[32]{0:T(128)S(1)}, f32[32]{0:T(128)}, u32[]{:S(2)}) copy-start(f32[32]{0:T(128)} %mul.91) | copy-start | bytes 388
  121.9 1.6 copy-start.3
  121.9 1.6 copy-start.12
  123.5 0.9 copy-start.7
  170.2 2.8 %copy-start.6 = (bf16[4,80,720]{2,1,0:T(8,128)(2,1)S(1)}, bf16[4,80,720]{2,1,0:T(8,128)(2,1)}, u32[]{:S(2)}) copy-start(bf16[4,80,720]{2,1,0:T(8,128)(2,1)} %param.12) | copy-start | bytes 1382404
  173.0 1.6 copy-start.5
where the time goes:
time: 177 us; the launch traced here: 176 us
  blocking collectives  56.8 us (32%)
  waiting for transfers between devices  50.7 us (29%)
  local copies, waits for them, and re-layouts  30.3 us (17%)
  starting transfers between devices  18.1 us (10%)
  matrix products  11.2 us (6%)
  other arithmetic  7.28 us (4%)
    all_to_all x1, blocking collectives, shards(): lax.all_to_all(back_lat, 'band', split_axis=2, concat_axis=3, tiled=True)  32.7 us
    all_to_all x1, waiting for transfers between devices, shards(): lax.all_to_all(along_lon, 'band', split_axis=3, concat_axis=2, tiled=True)  26.2 us
    all_to_all x1, waiting for transfers between devices, sum_at_owner(): lax.all_to_all(pieces, axis, split_axis=0, concat_axis=0, tiled=True)  24.6 us
    all_to_all x1, blocking collectives, from_everyone(): lax.all_to_all(jnp.broadcast_to(x[None], (devices, *x.shape)), axis, 0, 0...  24.1 us
    all_to_all x1, starting transfers between devices, sum_at_owner(): lax.all_to_all(pieces, axis, split_axis=0, concat_axis=0, tiled=True)  11.1 us
    all_to_all x1, starting transfers between devices, shards(): lax.all_to_all(along_lon, 'band', split_axis=3, concat_axis=2, tiled=True)  6.96 us
    convert_element_type x1, local copies, waits for them, and re-layouts, shards(): back_lat = jnp.einsum('ji,msjk->msik', lat_root, adjoints, preferred_elem...  6.66 us
    unnamed x33, local copies, waits for them, and re-layouts  5.99 us
  transfers between devices with their start and end apart: 2, of which 2 were waited for; matrix products, arithmetic and copies ran while one was open for 4% of the time, Pallas kernels for 0%

commit v1 on v0

v1 whole, which is shorter than its diff:
```python
import functools

import jax
import jax.numpy as jnp
import numpy as np
from jax import lax
from jax.experimental import pallas as pl
from jax.experimental.pallas import tpu as pltpu
from jax.sharding import PartitionSpec as P

MESH = pl.DeviceIdType.MESH
F32, BF16 = jnp.float32, jnp.bfloat16

S, CH, MEMB, FIELDS = 4, 32, 2, 3
ROWS, LAT, LON, COLS = 80, 320, 720, 180
REM = COLS - 128
QN, ZN, OWN, PAD = 8, 8, 5, 48
PERM = QN * PAD
PAIR, WIDE = 384, 768


def row_order():
    order = np.zeros((PERM, LAT), np.float32)
    for q in range(QN):
        for z in range(ZN):
            for k in range(OWN):
                order[q * PAD + z * OWN + k, 40 * z + 5 * q + k] = 1.0
    return order


def low_half(shape):
    return lax.broadcasted_iota(jnp.int32, shape, len(shape) - 1) < 64


def joined(even, odd):
    return jnp.where(low_half(even.shape), even, pltpu.roll(odd, 64, 1))


def joined_high(even, odd):
    return jnp.where(low_half(even.shape), pltpu.roll(even, 64, 1), odd)


def kernel(
    alpha_hbm, static_hbm, pert_hbm, std_hbm, w_hbm, lat_hbm, jac_hbm, count_hbm, mask_hbm, order_hbm, order_t_hbm,
    error_ref, weight_ref,
    ga_hbm, gs_hbm,
    alpha, static, pert, std, w, lat, jac, count, mask, order, order_t,
    fs, xr, ss, sr, rs, r1, s2, r2, gz, gzr, cbuf, ag, bs, br, lhs, out,
    spread, packed, rem, latp, latpt, incs, gu,
    load_sem, store_sem, f_send, f_recv, t_send, t_recv, a_send, a_recv, b_send, b_recv, c_send, c_recv, d_send, d_recv,
    e_send, e_recv,
):
    mem, band = lax.axis_index("mem"), lax.axis_index("band")
    z, q = mem // QN, lax.rem(mem, QN)

    bands = [lax.rem(band + k, 4) for k in range(1, 4)]
    to_band = [{"mem": mem, "band": b} for b in bands]
    qs = [lax.rem(q + k, QN) for k in range(1, QN)]
    to_q = [{"mem": z * QN + t, "band": band} for t in qs]
    zs = [lax.rem(z + k, ZN) for k in range(1, ZN)]
    to_z = [{"mem": t * QN + q, "band": band} for t in zs]

    staged = [(alpha_hbm, alpha), (w_hbm, w), (static_hbm, static), (lat_hbm, lat), (order_hbm, order),
              (order_t_hbm, order_t), (pert_hbm, pert), (std_hbm, std), (jac_hbm, jac), (count_hbm, count), (mask_hbm, mask)]
    loads = [pltpu.make_async_copy(src, dst, load_sem.at[i]) for i, (src, dst) in enumerate(staged)]
    for load in loads:
        load.start()

    barrier = pltpu.get_barrier_semaphore()
    partners = to_band + to_q + to_z
    for device in partners:
        pl.semaphore_signal(barrier, inc=1, device_id=device, device_id_type=MESH)

    def remote(src, dst, send, recv, device):
        return pltpu.make_async_remote_copy(
            src_ref=src, dst_ref=dst, send_sem=send, recv_sem=recv, device_id=device, device_id_type=MESH)

    sent = []

    forward = []
    loads[0].wait()
    loads[1].wait()
    for p in range(2):
        rows = alpha[:, 2 * p : 2 * p + 2].reshape(4 * ROWS, LON)
        y = jnp.dot(rows, w[...], preferred_element_type=F32).reshape(MEMB, 2, ROWS, WIDE)
        for m in range(MEMB):
            even, odd = y[m, 0], y[m, 1]
            for b in range(4):
                t = 512 + 128 * (b // 2)
                join = joined if b % 2 == 0 else joined_high
                fs[p, b, m, :, 0:128] = even[:, 128 * b : 128 * b + 128].astype(BF16)
                fs[p, b, m, :, 128:256] = odd[:, 128 * b : 128 * b + 128].astype(BF16)
                fs[p, b, m, :, 256:384] = join(even[:, t : t + 128], odd[:, t : t + 128]).astype(BF16)
        if p == 0:
            pl.semaphore_wait(barrier, len(partners))
        copies = [
            remote(fs.at[p, bands[k]], xr.at[p, :, band], f_send.at[p, k], f_recv.at[p, k], to_band[k]) for k in range(3)]
        for copy in copies:
            copy.start()
        forward.append(copies)
        xr[p, :, band] = fs[p, band]

    loads[2].wait()
    loads[3].wait()
    y = jnp.dot(static[...].reshape(S * ROWS, LON), w[...], preferred_element_type=F32).astype(BF16)
    own = (lax.broadcasted_iota(jnp.int32, (16, LAT), 1) == OWN * mem + lax.broadcasted_iota(jnp.int32, (16, LAT), 0)) & (
        lax.broadcasted_iota(jnp.int32, (16, LAT), 0) < OWN)
    own_rows = jnp.dot(jnp.where(own, 1.0, 0.0).astype(BF16), lat[...], preferred_element_type=F32).astype(BF16)
    here = lax.broadcasted_iota(jnp.int32, (LAT, ROWS), 0) == ROWS * band + lax.broadcasted_iota(jnp.int32, (LAT, ROWS), 1)
    own_part = jnp.dot(own_rows, jnp.where(here, 1.0, 0.0).astype(BF16), preferred_element_type=F32).astype(BF16)
    parts = [jnp.dot(own_part, y[ROWS * s : ROWS * s + ROWS], preferred_element_type=F32)[0:8] for s in range(S)]
    for b in range(4):
        t = 512 + 128 * (b // 2)
        join = joined if b % 2 == 0 else joined_high
        for p in range(2):
            for s in range(2):
                ss[b, :, PAIR * p + 128 * s : PAIR * p + 128 * s + 128] = parts[2 * p + s][:, 128 * b : 128 * b + 128]
            ss[b, :, PAIR * p + 256 : PAIR * p + 384] = join(parts[2 * p][:, t : t + 128], parts[2 * p + 1][:, t : t + 128])
    static_copies = [
        remote(ss.at[bands[k]], sr.at[band], t_send.at[k], t_recv.at[k], to_band[k]) for k in range(3)]
    for copy in static_copies:
        copy.start()
    sr[band] = ss[band]

    loads[4].wait()
    loads[5].wait()
    latp[...] = jnp.dot(order[...], lat[...], preferred_element_type=F32).astype(BF16)
    lat_t = jnp.transpose(lat[...].astype(F32)).astype(BF16)
    latpt[...] = jnp.dot(lat_t, order_t[...], preferred_element_type=F32).astype(BF16)
    weights = weight_ref[...].astype(F32)
    coef = weights / jnp.sqrt(jnp.sum(weights * weights, axis=1, keepdims=True))
    lane = lax.broadcasted_iota(jnp.int32, coef.shape, 1)
    rem[...] = jnp.zeros_like(rem)

    def pack(source):
        for p in range(2):
            for s in range(2):
                packed[:, PAIR * p + 128 * s : PAIR * p + 128 * s + 128] = source(2 * p + s, 0, 128).astype(F32)
                rem[s, :, 0:REM] = source(2 * p + s, 128, COLS).astype(F32)
            packed[:, PAIR * p + 256 : PAIR * p + 384] = joined(rem[0], rem[1])

    loads[6].wait()
    for m in range(MEMB):
        pack(lambda s, lo, hi: pert[m, s, :, lo:hi])
        factor = 0.8 * jnp.sum(jnp.where(lane == MEMB * mem + m, coef, 0.0), axis=1, keepdims=True)
        spread[m] = factor * jnp.dot(order[...], packed[...].astype(BF16), preferred_element_type=F32)
    loads[7].wait()
    pack(lambda s, lo, hi: std[s, :, lo:hi])
    spread[MEMB] = 0.6 * jnp.dot(
        order[...].astype(F32), packed[...], preferred_element_type=F32, precision=lax.Precision.HIGHEST)
    own_std = 0.6 * jnp.dot(
        jnp.where(own, 1.0, 0.0), packed[...], preferred_element_type=F32, precision=lax.Precision.HIGHEST)[0:8]

    first = []
    for p in range(2):
        for copy in forward[p]:
            copy.wait_recv()
        total = None
        for m in range(MEMB):
            field = jnp.dot(latp[...], xr[p, m].reshape(LAT, PAIR), preferred_element_type=F32)
            term = spread[m, :, PAIR * p : PAIR * p + PAIR] * field
            total = term if total is None else total + term
        rs[p] = total.astype(BF16).reshape(QN, PAD, PAIR)
        copies = [
            remote(rs.at[p, qs[k]], r1.at[p, k], a_send.at[p, k], a_recv.at[p, k], to_q[k]) for k in range(QN - 1)]
        for copy in copies:
            copy.start()
        first.append(copies)
        sent += forward[p]

    second = []
    for p in range(2):
        for copy in first[p]:
            copy.wait_recv()
        total = rs[p, q].astype(F32)
        for k in range(QN - 1):
            total = total + r1[p, k].astype(F32)
        for t in range(ZN):
            s2[p, t, 0:OWN, :] = total[OWN * t : OWN * t + OWN, :]
            s2[p, t, OWN:8, :] = jnp.zeros((8 - OWN, PAIR), F32)
        copies = [
            remote(s2.at[p, zs[k]], r2.at[p, k], b_send.at[p, k], b_recv.at[p, k], to_z[k]) for k in range(ZN - 1)]
        for copy in copies:
            copy.start()
        second.append(copies)
        sent += first[p]

    for copy in static_copies:
        copy.wait_recv()
    sent += static_copies
    own_static = sr[0] + sr[1] + sr[2] + sr[3]
    static_term = own_std * own_static
    loads[8].wait()
    loads[9].wait()
    loads[10].wait()
    for p in range(2):
        for copy in second[p]:
            copy.wait_recv()
        sent += second[p]
        total = s2[p, z]
        for k in range(ZN - 1):
            total = total + r2[p, k]
        total = total + static_term[:, PAIR * p : PAIR * p + PAIR]
        for s in range(2):
            incs[2 * p + s, :, 0:128] = total[:, 128 * s : 128 * s + 128]
            rest = total[:, 256:384]
            incs[2 * p + s, :, 128:256] = rest if s == 0 else pltpu.roll(rest, 64, 1)
    inc = [incs[s, 0:OWN, 0:COLS] for s in range(S)]
    counts = count[...].astype(F32)

    def channel(c, grads):
        jac_c = [jac[c, s].astype(F32) for s in range(S)]
        radiance = (jac_c[0] * inc[0] + jac_c[1] * inc[1]) + (jac_c[2] * inc[2] + jac_c[3] * inc[3])
        error = jnp.full((OWN, COLS), error_ref[c], F32)
        weighted = mask[c].astype(F32) * counts / (error * error) * radiance
        return tuple(grads[s] + jac_c[s] * weighted for s in range(S))

    grads = lax.fori_loop(0, CH, channel, tuple(jnp.zeros((OWN, COLS), F32) for _ in range(S)))
    gu[...] = jnp.zeros_like(gu)
    for s in range(S):
        gu[s, 0:OWN, 0:COLS] = grads[s].astype(BF16).astype(F32)
    for p in range(2):
        for s in range(2):
            gz[:, PAIR * p + 128 * s : PAIR * p + 128 * s + 128] = gu[2 * p + s, :, 0:128]
        gz[:, PAIR * p + 256 : PAIR * p + 384] = joined(gu[2 * p, :, 128:256], gu[2 * p + 1, :, 128:256])

    third = [remote(gz, gzr.at[z], c_send.at[k], c_recv.at[k], to_z[k]) for k in range(ZN - 1)]
    for copy in third:
        copy.start()
    gzr[z] = gz[...]
    for copy in third:
        copy.wait_recv()
    sent += third
    for t in range(ZN):
        cbuf[OWN * t : OWN * t + OWN, :] = gzr[t, 0:OWN, :]
    cbuf[OWN * ZN : PAD, :] = jnp.zeros((PAD - OWN * ZN, WIDE), F32)
    ag[q] = cbuf[...].astype(BF16)
    fourth = [remote(ag.at[q], ag.at[q], d_send.at[k], d_recv.at[k], to_q[k]) for k in range(QN - 1)]
    for copy in fourth:
        copy.start()
    for copy in fourth:
        copy.wait_recv()
    sent += fourth

    gradient = ag[...].reshape(PERM, WIDE).astype(F32)
    back = []
    for m in range(FIELDS):
        adjoint = (spread[m] * gradient).astype(BF16)
        bs[m] = jnp.dot(latpt[...], adjoint, preferred_element_type=F32).astype(BF16).reshape(4, ROWS, WIDE)
        copies = [
            remote(bs.at[m, bands[k]], br.at[m, band], e_send.at[m, k], e_recv.at[m, k], to_band[k]) for k in range(3)]
        for copy in copies:
            copy.start()
        back.append(copies)
        br[m, band] = bs[m, band]

    stores = []
    for m in range(FIELDS):
        for copy in back[m]:
            copy.wait_recv()
        sent += back[m]
        for p in range(2):
            tiles = [br[m, b, :, PAIR * p + 256 : PAIR * p + 384].astype(F32) for b in range(4)]
            for s in range(2):
                rows = pl.ds((2 * p + s) * ROWS, ROWS)
                for b in range(4):
                    lhs[rows, 128 * b : 128 * b + 128] = br[m, b, :, PAIR * p + 128 * s : PAIR * p + 128 * s + 128]
                join = joined if s == 0 else joined_high
                for t in range(2):
                    lhs[rows, 512 + 128 * t : 640 + 128 * t] = join(tiles[2 * t], tiles[2 * t + 1]).astype(BF16)
        y = lax.dot_general(lhs[...], w[...], (((1,), (1,)), ((), ())), preferred_element_type=F32)
        base = alpha[m] if m < MEMB else static[...]
        out[m] = base.astype(F32) + y.reshape(S, ROWS, LON)
        store = pltpu.make_async_copy(out.at[m], ga_hbm.at[m] if m < MEMB else gs_hbm, store_sem.at[m])
        store.start()
        stores.append(store)
    for store in stores:
        store.wait()
    for copy in sent:
        copy.wait_send()


def shards(alpha, static_ctl, perturbations, static_std, lon_root, lat_root, jacobian, obs_count, channel_mask,
           channel_error, member_weight):
    pieces = [lon_root[:, COLS * b : COLS * b + 128] for b in range(4)]
    for b in range(4):
        pieces += [lon_root[:, COLS * b + 128 : COLS * b + COLS], jnp.zeros((LON, 64 - REM), BF16)]
    w = jnp.concatenate(pieces, axis=1)
    order = row_order()
    any_space = pl.BlockSpec(memory_space=pl.ANY)
    inputs = [alpha, static_ctl, perturbations, static_std, w, lat_root, jacobian, obs_count, channel_mask,
              jnp.asarray(order, BF16), jnp.asarray(order.T, BF16)]
    dma = pltpu.SemaphoreType.DMA
    vmem = pltpu.VMEM
    scratch = [vmem(x.shape, x.dtype) for x in inputs] + [
        vmem((2, 4, MEMB, ROWS, PAIR), BF16),
        vmem((2, MEMB, 4, ROWS, PAIR), BF16),
        vmem((4, 8, WIDE), F32),
        vmem((4, 8, WIDE), F32),
        vmem((2, QN, PAD, PAIR), BF16),
        vmem((2, QN - 1, PAD, PAIR), BF16),
        vmem((2, ZN, 8, PAIR), F32),
        vmem((2, ZN - 1, 8, PAIR), F32),
        vmem((8, WIDE), F32),
        vmem((ZN, 8, WIDE), F32),
        vmem((PAD, WIDE), F32),
        vmem((QN, PAD, WIDE), BF16),
        vmem((FIELDS, 4, ROWS, WIDE), BF16),
        vmem((FIELDS, 4, ROWS, WIDE), BF16),
        vmem((S * ROWS, WIDE), BF16),
        vmem((FIELDS, S, ROWS, LON), F32),
        vmem((FIELDS, PERM, WIDE), F32),
        vmem((LAT, WIDE), F32),
        vmem((2, LAT, 128), F32),
        vmem((PERM, LAT), BF16),
        vmem((LAT, PERM), BF16),
        vmem((S, 8, 256), F32),
        vmem((S, 8, 256), F32),
        dma((len(inputs),)), dma((FIELDS,)),
        dma((2, 3)), dma((2, 3)), dma((3,)), dma((3,)),
        dma((2, QN - 1)), dma((2, QN - 1)), dma((2, ZN - 1)), dma((2, ZN - 1)),
        dma((ZN - 1,)), dma((ZN - 1,)), dma((QN - 1,)), dma((QN - 1,)),
        dma((FIELDS, 3)), dma((FIELDS, 3)),
    ]
    return pl.pallas_call(
        kernel,
        out_shape=(jax.ShapeDtypeStruct((MEMB, S, ROWS, LON), F32), jax.ShapeDtypeStruct((S, ROWS, LON), F32)),
        in_specs=[any_space] * len(inputs)
        + [pl.BlockSpec(memory_space=pltpu.SMEM), pl.BlockSpec(memory_space=pltpu.VMEM)],
        out_specs=(any_space, any_space),
        scratch_shapes=scratch,
        compiler_params=pltpu.CompilerParams(collective_id=0, has_side_effects=True, vmem_limit_bytes=48 << 20),
        name="hessian",
    )(*inputs, channel_error, member_weight.reshape(1, -1))


def solution(mesh):
    in_specs = (
        P("mem", None, "band", None),
        P(None, "band", None),
        P("mem", None, None, "band"),
        P(None, None, "band"),
        P(),
        P(),
        P(None, None, "mem", "band"),
        P("mem", "band"),
        P(None, "mem", "band"),
        P(),
        P(),
    )
    out_specs = (P("mem", None, "band", None), P(None, "band", None))
    return jax.shard_map(shards, mesh=mesh, in_specs=in_specs, out_specs=out_specs, check_vma=False)
```

time: 177 us -> 91.4 us (0.52)
  the two profiles are of different devices: /device:TPU:1 before, /device:TPU:37 now
where the time goes in v1:
time: 91.4 us; the launch traced here: 91 us
  Pallas kernels  71.2 us (78%)
  local copies, waits for them, and re-layouts  19.1 us (21%)
    pallas_call x1, Pallas kernels, shards(): pl.pallas_call(kernel, out_shape=(jax.ShapeDtypeStruct((MEMB, S, ROWS, LO...  71.2 us
    unnamed x26, local copies, waits for them, and re-layouts  13.9 us
    concatenate x1, local copies, waits for them, and re-layouts, shards(): w = jnp.concatenate(pieces, axis=1)  3.16 us

profile of v1, /device:TPU:37, one launch (start us, length us, event | category | flops | bytes accessed | tf_op | source)
XLA Modules:
  0.0 91.0 jit_solution(6831189181814124546)
XLA Ops:
  0.6 0.0 copy-start.8
  0.6 1.1 %copy.18.mask_hbm = s32[32,5,180]{2,1,0:T(8,128)S(1)} copy(s32[32,5,180]{2,0,1:T(8,128)} %param.21) | data formatting | bytes 230400 | tf_op args[8]
  1.8 1.1 %copy.17.jac_hbm = bf16[32,4,5,180]{3,2,1,0:T(8,128)(2,1)S(1)} copy(bf16[32,4,5,180]{3,1,2,0:T(4,128)(2,1)} %param.19) | data formatting | bytes 460800 | tf_op args[6]
  2.8 0.0 copy-done.8
  2.8 0.9 %fusion = (bf16[720,52]{1,0:T(8,128)(2,1)S(1)}, bf16[720,52]{1,0:T(8,128)(2,1)S(1)}, bf16[720,52]{1,0:T(8,128)(2,1)}, bf16[720,52]{1,0:T(8,128)(2,1)}) fusion(bf16[720,720]{1,0:T(8,128)(2,1)S(1)} %copy-done.8), kind=kLoop, calls=%fused_computation | loop fusion | bytes 599040 | tf_op jit(solution)/shard_map/slice | solution.py:287
  3.8 1.1 %fusion.1 = (bf16[720,128]{1,0:T(8,128)(2,1)}, bf16[720,128]{1,0:T(8,128)(2,1)}, bf16[720,128]{1,0:T(8,128)(2,1)}, bf16[720,128]{1,0:T(8,128)(2,1)}) fusion(bf16[720,720]{1,0:T(8,128)(2,1)S(1)} %copy-done.8), kind=kLoop, calls=%fused_computation.1 | loop fusion | bytes 1474560 | tf_op jit(solution)/shard_map/slice | solution.py:285
  4.8 0.0 copy-start.9
  4.9 3.2 %concatenate.3.w_hbm = bf16[720,768]{1,0:T(8,128)(2,1)S(1)} concatenate(bf16[720,128]{1,0:T(8,128)(2,1)} %get-tuple-element.9, bf16[720,128]{1,0:T(8,128)(2,1)} %get-tuple-element.8, bf16[720,128]{1,0:T(8,128)(2,1)} %get-tuple-element.7, bf16[720,128]{1,0:T(8,128)(2,1)} %get-tuple-element.6, bf16[720,52]{1,0:T(8,128)(2,1)} %get-tuple-element.4, bf16[720,12]{1,0:T(8,128)(2,1)S(1)} %broadcast.3, ...), dimensions={1} | concatenate | bytes 2211840 | tf_op jit(solution)/shard_map/concatenate | solution.py:288
  8.0 0.0 copy-done.9
  8.0 2.3 %copy.15.pert_hbm = bf16[2,4,320,180]{3,2,1,0:T(8,128)(2,1)} copy(bf16[2,4,320,180]{2,1,3,0:T(4,128)(2,1)S(1)} %copy-done.9) | data formatting | bytes 1843200 | tf_op args[2]
  10.3 0.0 copy-start.7
  10.3 2.7 %copy.16.std_hbm = f32[4,320,180]{2,1,0:T(8,128)} copy(f32[4,320,180]{1,0,2:T(4,128)} %param.16) | data formatting | bytes 1843200 | tf_op args[3]
  13.0 0.0 copy-done
  13.0 0.0 copy-done.1
  13.0 0.0 copy-done.5
  13.0 0.0 copy-done.6
  13.1 0.0 copy-done.7
  13.1 0.0 copy-start.2
  13.1 1.0 %copy-done.2 = bf16[384,320]{1,0:T(8,128)(2,1)S(1)} copy-done((bf16[384,320]{1,0:T(8,128)(2,1)S(1)}, bf16[384,320]{1,0:T(8,128)(2,1)}, u32[]{:S(2)}) %copy-start.2) | copy-done | bytes 245784
  14.0 0.9 %copy-done.3 = bf16[320,320]{1,0:T(8,128)(2,1)S(1)} copy-done((bf16[320,320]{1,0:T(8,128)(2,1)S(1)}, bf16[320,320]{1,0:T(8,128)(2,1)}, u32[]{:S(2)}) %copy-start.3) | copy-done | bytes 204824
  15.0 0.9 %copy-done.4 = bf16[320,384]{1,0:T(8,128)(2,1)S(1)} copy-done((bf16[320,384]{1,0:T(8,128)(2,1)S(1)}, bf16[320,384]{1,0:T(8,128)(2,1)}, u32[]{:S(2)}) %copy-start.4) | copy-done | bytes 245784
  15.9 71.2 %hessian.1 = (f32[2,4,80,720]{3,2,1,0:T(8,128)}, f32[4,80,720]{2,1,0:T(8,128)S(1)}) custom-call(bf16[2,4,80,720]{3,2,1,0:T(8,128)(2,1)S(1)} %copy-done, bf16[4,80,720]{2,1,0:T(8,128)(2,1)S(1)} %copy-done.1, bf16[2,4,320,180]{3,2,1,0:T(8,128)(2,1)} %copy.15.pert_hbm, f32[4,320,180]{2,1,0:T(8,128)} %copy.16.std_hbm, bf16[720,768]{1,0:T(8,128)(2,1)S(1)} %concatenate.3.w_hbm, ...), custom_call_target="tpu_custom_call" | custom-call | tf_op jit(solution)/shard_map/hessian/pallas_call | solution.py:325
  87.1 3.0 %copy.21 = f32[2,4,80,720]{3,2,1,0:T(8,128)} copy(f32[2,4,80,720]{3,2,1,0:T(8,128)} %get-tuple-element.12) | data formatting | bytes 3686400
  90.1 0.9 %copy.22 = f32[4,80,720]{2,1,0:T(8,128)} copy(f32[4,80,720]{2,1,0:T(8,128)S(1)} %get-tuple-element.13) | data formatting | bytes 1843200
  (7 shorter events, 0.0 us)
Async XLA Ops:
  0.6 2.2 %copy-start.8 = (bf16[720,720]{1,0:T(8,128)(2,1)S(1)}, bf16[720,720]{1,0:T(8,128)(2,1)}, u32[]{:S(2)}) copy-start(bf16[720,720]{1,0:T(8,128)(2,1)} %param.17) | copy-start | bytes 3110404
  4.8 3.2 %copy-start.9 = (bf16[2,4,320,180]{2,1,3,0:T(4,128)(2,1)S(1)}, bf16[2,4,320,180]{2,1,3,0:T(4,128)(2,1)}, u32[]{:S(2)}) copy-start(bf16[2,4,320,180]{2,1,3,0:T(4,128)(2,1)} %param.15) | copy-start | bytes 2764804
  10.3 2.7 %copy-start = (bf16[2,4,80,720]{3,2,1,0:T(8,128)(2,1)S(1)}, bf16[2,4,80,720]{3,2,1,0:T(8,128)(2,1)}, u32[]{:S(2)}) copy-start(bf16[2,4,80,720]{3,2,1,0:T(8,128)(2,1)} %alpha_hbm.1) | copy-start | bytes 2764804
  10.3 2.7 %copy-start.1 = (bf16[4,80,720]{2,1,0:T(8,128)(2,1)S(1)}, bf16[4,80,720]{2,1,0:T(8,128)(2,1)}, u32[]{:S(2)}) copy-start(bf16[4,80,720]{2,1,0:T(8,128)(2,1)} %static_hbm.1) | copy-start | bytes 1382404
  10.3 2.7 %copy-start.5 = (s32[5,180]{1,0:T(8,128)S(1)}, s32[5,180]{1,0:T(8,128)}, u32[]{:S(2)}) copy-start(s32[5,180]{1,0:T(8,128)} %count_hbm.1) | copy-start | bytes 10804
  10.3 2.7 %copy-start.6 = (f32[32]{0:T(128)S(1)}, f32[32]{0:T(128)}, u32[]{:S(2)}) copy-start(f32[32]{0:T(128)} %error_ref.1) | copy-start | bytes 388
  10.3 2.7 %copy-start.7 = (s32[128]{0:T(128)S(1)}, s32[128]{0:T(128)}, u32[]{:S(2)}) copy-start(s32[128]{0:T(128)} %param.23) | copy-start | bytes 1540
  13.1 1.0 %copy-start.2 = (bf16[384,320]{1,0:T(8,128)(2,1)S(1)}, bf16[384,320]{1,0:T(8,128)(2,1)}, u32[]{:S(2)}) copy-start(bf16[384,320]{1,0:T(8,128)(2,1)} %constant.6.clone.order_hbm) | copy-start | bytes 737284
  14.0 0.9 %copy-start.3 = (bf16[320,320]{1,0:T(8,128)(2,1)S(1)}, bf16[320,320]{1,0:T(8,128)(2,1)}, u32[]{:S(2)}) copy-start(bf16[320,320]{1,0:T(8,128)(2,1)} %lat_hbm.1) | copy-start | bytes 614404
  15.0 0.9 %copy-start.4 = (bf16[320,384]{1,0:T(8,128)(2,1)S(1)}, bf16[320,384]{1,0:T(8,128)(2,1)}, u32[]{:S(2)}) copy-start(bf16[320,384]{1,0:T(8,128)(2,1)} %constant.7.clone.order_t_hbm) | copy-start | bytes 737284

commit v2 on v1

v2 whole, which is shorter than its diff:
```python
import functools

import jax
import jax.numpy as jnp
from jax import lax
from jax.experimental import pallas as pl
from jax.experimental.pallas import tpu as pltpu
from jax.sharding import PartitionSpec as P

MESH = pl.DeviceIdType.MESH
F32, BF16, I32 = jnp.float32, jnp.bfloat16, jnp.int32

S, CH, MEMB, FIELDS = 4, 32, 2, 3
ROWS, LAT, LON, COLS = 80, 320, 720, 180
REM = COLS - 128
YN, TN, OWN = 4, 16, 5
PAIR, WIDE = 384, 768
PIECE = 16


def iota(shape, dim):
    return lax.broadcasted_iota(I32, shape, dim)


def one_hot(rows, columns, column_of_row):
    return jnp.where(iota((rows, columns), 1) == column_of_row(iota((rows, columns), 0)), 1.0, 0.0).astype(BF16)


def fifth(x):
    return (x * 205) // 1024


def grid_row(p):
    y = p // ROWS
    t = fifth(p - ROWS * y)
    return OWN * (8 * (t // 2) + 4 * (t % 2) + y) + p - ROWS * y - OWN * t


def packed_lane(row):
    j, s = row // 4, row % 4
    tail = jnp.where(j < 128, 128 * (s % 2) + j, 256 + 64 * (s % 2) + j - 128)
    return PAIR * (s // 2) + tail


def piece_row(a):
    t, r = a // PIECE, a % PIECE
    tile = fifth(r)
    return jnp.where(r < 3 * OWN, ROWS * tile + OWN * t + r - OWN * tile, -1)


def low_half(shape):
    return iota(shape, len(shape) - 1) < 64


def joined(even, odd):
    return jnp.where(low_half(even.shape), even, pltpu.roll(odd, 64, 1))


def joined_high(even, odd):
    return jnp.where(low_half(even.shape), pltpu.roll(even, 64, 1), odd)


def dot(a, b, contract=(1, 0)):
    return lax.dot_general(a, b, (((contract[0],), (contract[1],)), ((), ())), preferred_element_type=F32)


def kernel(
    alpha_hbm, static_hbm, pert_hbm, std_hbm, lon_hbm, lat_hbm, jac_hbm, count_hbm, mask_hbm, error_ref, weight_ref,
    ga_hbm, gs_hbm,
    alpha, static, pert, std, lon, lat, jac, count, mask,
    w, fs, rl, xr, ss, sr, rs, r1, s2, r2, gp, gzr, ag, bs, bl, br, lhs, out,
    spread, packed, rem, order, latp, latpt, spreader, to_piece, from_piece, squares, terms, isc, gsc, incs,
    load_sem, std_sem, store_sem, f_send, f_recv, t_send, t_recv, a_send, a_recv, b_send, b_recv, c_send, c_recv,
    d_send, d_recv, e_send, e_recv,
):
    mem, band = lax.axis_index("mem"), lax.axis_index("band")
    z, x, y = mem // 8, (mem // 4) % 2, mem % 4
    t = 2 * z + x
    chip, core = band // 2, band % 2
    sib, far, cross = 2 * chip + 1 - core, 2 * (1 - chip) + core, 3 - band

    def at_band(b):
        return {"mem": mem, "band": b}

    ys = [lax.rem(y + k, YN) for k in range(1, YN)]
    to_y = [{"mem": 8 * z + 4 * x + v, "band": band} for v in ys]
    ts = [lax.rem(t + k, TN) for k in range(1, TN)]
    to_t = [{"mem": 8 * (v // 2) + 4 * (v % 2) + y, "band": band} for v in ts]

    staged = [(lon_hbm, lon), (alpha_hbm, alpha), (static_hbm, static), (lat_hbm, lat),
              (pert_hbm.reshape(MEMB, S * COLS, LAT), pert), (jac_hbm, jac), (count_hbm, count), (mask_hbm, mask)]
    loads = [pltpu.make_async_copy(src, dst, load_sem.at[i]) for i, (src, dst) in enumerate(staged)]
    loads += [pltpu.make_async_copy(std_hbm.at[:, s, :], std.at[s], std_sem.at[s]) for s in range(S)]
    for load in loads:
        load.start()

    barrier = pltpu.get_barrier_semaphore()
    partners = [at_band(sib), at_band(far)] + to_y + to_t
    for device in partners:
        pl.semaphore_signal(barrier, inc=1, device_id=device, device_id_type=MESH)

    def remote(src, dst, send, recv, device):
        return pltpu.make_async_remote_copy(
            src_ref=src, dst_ref=dst, send_sem=send, recv_sem=recv, device_id=device, device_id_type=MESH)

    sent = []

    loads[0].wait()
    for b in range(4):
        w[:, 128 * b : 128 * b + 128] = lon[:, COLS * b : COLS * b + 128]
        w[:, 512 + 64 * b : 512 + 64 * b + REM] = lon[:, COLS * b + 128 : COLS * b + COLS]
        w[:, 512 + 64 * b + REM : 576 + 64 * b] = jnp.zeros((LON, 64 - REM), BF16)

    forward = []
    loads[1].wait()
    for p in range(2):
        rows = alpha[:, 2 * p : 2 * p + 2].reshape(4 * ROWS, LON)
        v = dot(rows, w[...]).reshape(MEMB, 2, ROWS, WIDE)
        for m in range(MEMB):
            even, odd = v[m, 0], v[m, 1]
            for b in range(4):
                tile = 512 + 128 * (b // 2)
                join = joined if b % 2 == 0 else joined_high
                fs[p, b, m, :, 0:128] = even[:, 128 * b : 128 * b + 128].astype(BF16)
                fs[p, b, m, :, 128:256] = odd[:, 128 * b : 128 * b + 128].astype(BF16)
                fs[p, b, m, :, 256:384] = join(even[:, tile : tile + 128], odd[:, tile : tile + 128]).astype(BF16)
        copies = [
            remote(fs.at[p, far], xr.at[p, :, band], f_send.at[p, 0], f_recv.at[p, 0], at_band(far)),
            remote(fs.at[p, cross], rl.at[p], f_send.at[p, 1], f_recv.at[p, 1], at_band(sib)),
            remote(fs.at[p, sib], xr.at[p, :, band], f_send.at[p, 2], f_recv.at[p, 2], at_band(sib)),
            remote(rl.at[p], xr.at[p, :, sib], f_send.at[p, 3], f_recv.at[p, 3], at_band(far)),
        ]
        if p == 0:
            pl.semaphore_wait(barrier, len(partners))
        else:
            forward[0][1].wait_recv()
            forward[0][3].start()
        for copy in copies[:3]:
            copy.start()
        forward.append(copies)
        xr[p, :, band] = fs[p, band]

    loads[2].wait()
    loads[3].wait()
    v = dot(static[...].reshape(S * ROWS, LON), w[...]).astype(BF16)
    forward[1][1].wait_recv()
    forward[1][3].start()
    own_rows = dot(one_hot(16, LAT, lambda k: jnp.where(k < OWN, OWN * mem + k, -1)), lat[...]).astype(BF16)
    here = jnp.where(iota((LAT, ROWS), 0) == ROWS * band + iota((LAT, ROWS), 1), 1.0, 0.0).astype(BF16)
    own_part = dot(own_rows, here).astype(BF16)
    parts = [dot(own_part, v[ROWS * s : ROWS * s + ROWS])[0:8] for s in range(S)]
    for b in range(4):
        tile = 512 + 128 * (b // 2)
        join = joined if b % 2 == 0 else joined_high
        for p in range(2):
            for s in range(2):
                ss[b, :, PAIR * p + 128 * s : PAIR * p + 128 * s + 128] = parts[2 * p + s][:, 128 * b : 128 * b + 128]
            ss[b, :, PAIR * p + 256 : PAIR * p + 384] = join(
                parts[2 * p][:, tile : tile + 128], parts[2 * p + 1][:, tile : tile + 128])
    static_copies = [
        remote(ss.at[far], sr.at[band], t_send.at[0], t_recv.at[0], at_band(far)),
        remote(ss.at[sib], sr.at[band], t_send.at[1], t_recv.at[1], at_band(sib)),
        remote(ss.at[cross], sr.at[4], t_send.at[2], t_recv.at[2], at_band(sib)),
        remote(sr.at[4], sr.at[sib], t_send.at[3], t_recv.at[3], at_band(far)),
    ]
    for copy in static_copies[:3]:
        copy.start()
    sr[band] = ss[band]

    order[...] = one_hot(LAT, LAT, grid_row)
    latp[...] = dot(order[...], lat[...]).astype(BF16)
    spreader[...] = one_hot(S * COLS, WIDE, packed_lane)
    weights = weight_ref[...].astype(F32)
    coef = weights / jnp.sqrt(jnp.sum(weights * weights, axis=1, keepdims=True))
    loads[4].wait()
    for m in range(MEMB):
        factor = 0.8 * jnp.sum(jnp.where(iota(coef.shape, 1) == MEMB * mem + m, coef, 0.0), axis=1, keepdims=True)
        ordered = dot(order[...], pert[m], (1, 1)).astype(BF16)
        spread[m, 0:LAT] = factor * dot(ordered, spreader[...])
    to_piece[...] = one_hot(TN * PIECE, 3 * ROWS, piece_row)
    static_copies[2].wait_recv()
    static_copies[3].start()

    first = []
    for p in range(2):
        for k in (0, 2, 3):
            forward[p][k].wait_recv()
        total = None
        for m in range(MEMB):
            term = spread[m, 0:LAT, PAIR * p : PAIR * p + PAIR] * dot(latp[...], xr[p, m].reshape(LAT, PAIR))
            total = term if total is None else total + term
        rs[p] = total.astype(BF16).reshape(YN, ROWS, PAIR)
        copies = [
            remote(rs.at[p, ys[k]], r1.at[p, k], a_send.at[p, k], a_recv.at[p, k], to_y[k]) for k in range(YN - 1)]
        for copy in copies:
            copy.start()
        first.append(copies)
        sent += forward[p]

    for load in loads[8:]:
        load.wait()
    rem[...] = jnp.zeros_like(rem)
    for p in range(2):
        for s in range(2):
            value = std[2 * p + s]
            ordered = None
            for _ in range(3):
                head = value.astype(BF16)
                term = dot(order[...], head, (1, 1))
                ordered = term if ordered is None else ordered + term
                value = value - head.astype(F32)
            ordered = 0.6 * ordered
            spread[MEMB, 0:LAT, PAIR * p + 128 * s : PAIR * p + 128 * s + 128] = ordered[:, 0:128]
            rem[s, :, 0:REM] = ordered[:, 128:COLS]
        spread[MEMB, 0:LAT, PAIR * p + 256 : PAIR * p + 384] = joined(rem[0], rem[1])
    latpt[...] = dot(jnp.transpose(lat[...].astype(F32)).astype(BF16), order[...], (1, 1)).astype(BF16)
    hot = iota((3 * ROWS, TN * PIECE), 0) == piece_row(iota((3 * ROWS, TN * PIECE), 1))
    from_piece[...] = jnp.where(hot, 1.0, 0.0).astype(BF16)
    error = jnp.sum(jnp.where(iota((CH, CH), 0) == iota((CH, CH), 1), error_ref[...], 0.0), axis=1, keepdims=True)
    squares[...] = jnp.broadcast_to(error * error, squares.shape)
    spread[:, LAT:] = jnp.zeros((FIELDS, 8, WIDE), F32)
    first_row = ROWS * y + OWN * t
    shift = first_row % 8
    own_std = spread[MEMB, pl.ds(pl.multiple_of(first_row - shift, 8), 16), :]
    own_std = pltpu.roll(own_std, (16 - shift) % 16, 0)[0:8]
    for k in (0, 1, 3):
        static_copies[k].wait_recv()
    sent += static_copies
    static_term = own_std * (sr[0] + sr[1] + sr[2] + sr[3])
    terms[...] = jnp.zeros_like(terms)
    for p in range(2):
        for l in range(3):
            terms[p, OWN * l : OWN * l + OWN] = static_term[0:OWN, PAIR * p + 128 * l : PAIR * p + 128 * l + 128]

    second = []
    for p in range(2):
        for copy in first[p]:
            copy.wait_recv()
        total = rs[p, y].astype(F32)
        for k in range(YN - 1):
            total = total + r1[p, k].astype(F32)
        total = total.astype(BF16)
        tall = jnp.concatenate([total[:, 0:128], total[:, 128:256], total[:, 256:384]], axis=0)
        s2[p] = dot(to_piece[...], tall).astype(BF16).reshape(TN, PIECE, 128)
        copies = [
            remote(s2.at[p, ts[k]], r2.at[p, k], b_send.at[p, k], b_recv.at[p, k], to_t[k]) for k in range(TN - 1)]
        for copy in copies:
            copy.start()
        second.append(copies)
        sent += first[p]

    for load in loads[5:8]:
        load.wait()
    for p in range(2):
        for copy in second[p]:
            copy.wait_recv()
        sent += second[p]
        total = terms[p] + s2[p, t].astype(F32)
        for k in range(TN - 1):
            total = total + r2[p, k].astype(F32)
        isc[2 * p, 0:OWN, 0:128] = total[0:OWN]
        isc[2 * p + 1, 0:OWN, 0:128] = total[OWN : 2 * OWN]
        isc[2 * p, 0:OWN, 128:256] = total[2 * OWN : 3 * OWN]
        isc[2 * p + 1, 0:OWN, 128:256] = pltpu.roll(total, 64, 1)[2 * OWN : 3 * OWN]
    for i in range(OWN):
        for s in range(S):
            incs[i, s : s + 1, :] = isc[s, i : i + 1, :]
    inc = [incs[i, 0:S, 0:COLS] for i in range(OWN)]
    counts = count[...].astype(F32)

    def channels(step, grads):
        base = pl.multiple_of(8 * step, 8)
        square = squares[pl.ds(base, 8), 0:1]
        grads = list(grads)
        for i in range(OWN):
            weight = mask[i, pl.ds(base, 8), :].astype(F32) * counts[i : i + 1, :] / square
            for c in range(8):
                jac_c = jac[base + c, i].astype(F32)
                radiance = jnp.sum(jac_c * inc[i], axis=0, keepdims=True)
                grads[i] = grads[i] + jac_c * (weight[c : c + 1, :] * radiance)
        return tuple(grads)

    grads = lax.fori_loop(0, CH // 8, channels, tuple(jnp.zeros((S, COLS), F32) for _ in range(OWN)))
    gsc[...] = jnp.zeros_like(gsc)
    for i in range(OWN):
        for s in range(S):
            gsc[s, i : i + 1, 0:COLS] = grads[i][s : s + 1, :].astype(BF16).astype(F32)
    for p in range(2):
        both = joined(gsc[2 * p, :, 128:256], gsc[2 * p + 1, :, 128:256])
        piece = [gsc[2 * p, 0:OWN, 0:128], gsc[2 * p + 1, 0:OWN, 0:128], both[0:OWN], jnp.zeros((1, 128), F32)]
        gp[p] = jnp.concatenate(piece, axis=0).astype(BF16)

    third = [remote(gp, gzr.at[:, t], c_send.at[k], c_recv.at[k], to_t[k]) for k in range(TN - 1)]
    for copy in third:
        copy.start()
    for p in range(2):
        gzr[p, t] = gp[p]
    for copy in third:
        copy.wait_recv()
    sent += third
    for p in range(2):
        tall = dot(from_piece[...], gzr[p].reshape(TN * PIECE, 128)).astype(BF16)
        for l in range(3):
            ag[y, :, PAIR * p + 128 * l : PAIR * p + 128 * l + 128] = tall[ROWS * l : ROWS * l + ROWS]
    fourth = [remote(ag.at[y], ag.at[y], d_send.at[k], d_recv.at[k], to_y[k]) for k in range(YN - 1)]
    for copy in fourth:
        copy.start()
    for copy in fourth:
        copy.wait_recv()
    sent += fourth

    gradient = ag[...].reshape(LAT, WIDE).astype(F32)
    back = []
    for m in range(FIELDS):
        adjoint = (spread[m, 0:LAT] * gradient).astype(BF16)
        bs[m] = dot(latpt[...], adjoint).astype(BF16).reshape(4, ROWS, WIDE)
        copies = [
            remote(bs.at[m, far], br.at[m, band], e_send.at[m, 0], e_recv.at[m, 0], at_band(far)),
            remote(bs.at[m, cross], bl.at[m], e_send.at[m, 1], e_recv.at[m, 1], at_band(sib)),
            remote(bs.at[m, sib], br.at[m, band], e_send.at[m, 2], e_recv.at[m, 2], at_band(sib)),
            remote(bl.at[m], br.at[m, sib], e_send.at[m, 3], e_recv.at[m, 3], at_band(far)),
        ]
        if m > 0:
            back[m - 1][1].wait_recv()
            back[m - 1][3].start()
        for copy in copies[:3]:
            copy.start()
        back.append(copies)
        br[m, band] = bs[m, band]
    back[FIELDS - 1][1].wait_recv()
    back[FIELDS - 1][3].start()

    stores = []
    for m in range(FIELDS):
        for k in (0, 2, 3):
            back[m][k].wait_recv()
        sent += back[m]
        for p in range(2):
            tiles = [br[m, b, :, PAIR * p + 256 : PAIR * p + 384].astype(F32) for b in range(4)]
            for s in range(2):
                rows = pl.ds((2 * p + s) * ROWS, ROWS)
                for b in range(4):
                    lhs[rows, 128 * b : 128 * b + 128] = br[m, b, :, PAIR * p + 128 * s : PAIR * p + 128 * s + 128]
                join = joined if s == 0 else joined_high
                for h in range(2):
                    lhs[rows, 512 + 128 * h : 640 + 128 * h] = join(tiles[2 * h], tiles[2 * h + 1]).astype(BF16)
        v = dot(lhs[...], w[...], (1, 1))
        base = alpha[m] if m < MEMB else static[...]
        out[m] = base.astype(F32) + v.reshape(S, ROWS, LON)
        store = pltpu.make_async_copy(out.at[m], ga_hbm.at[m] if m < MEMB else gs_hbm, store_sem.at[m])
        store.start()
        stores.append(store)
    for store in stores:
        store.wait()
    for copy in sent:
        copy.wait_send()


def shards(alpha, static_ctl, perturbations, static_std, lon_root, lat_root, jacobian, obs_count, channel_mask,
           channel_error, member_weight):
    inputs = [alpha, static_ctl, jnp.transpose(perturbations, (0, 3, 1, 2)), jnp.transpose(static_std, (2, 0, 1)),
              lon_root, lat_root, jnp.transpose(jacobian, (0, 2, 1, 3)), obs_count, jnp.transpose(channel_mask, (1, 0, 2))]
    dma, vmem = pltpu.SemaphoreType.DMA, pltpu.VMEM
    scratch = [
        vmem((MEMB, S, ROWS, LON), BF16),
        vmem((S, ROWS, LON), BF16),
        vmem((MEMB, S * COLS, LAT), BF16),
        vmem((S, COLS, LAT), F32),
        vmem((LON, LON), BF16),
        vmem((LAT, LAT), BF16),
        vmem((CH, OWN, S, COLS), BF16),
        vmem((OWN, COLS), I32),
        vmem((OWN, CH, COLS), I32),
        vmem((LON, WIDE), BF16),
        vmem((2, 4, MEMB, ROWS, PAIR), BF16),
        vmem((2, MEMB, ROWS, PAIR), BF16),
        vmem((2, MEMB, 4, ROWS, PAIR), BF16),
        vmem((4, 8, WIDE), F32),
        vmem((5, 8, WIDE), F32),
        vmem((2, YN, ROWS, PAIR), BF16),
        vmem((2, YN - 1, ROWS, PAIR), BF16),
        vmem((2, TN, PIECE, 128), BF16),
        vmem((2, TN - 1, PIECE, 128), BF16),
        vmem((2, PIECE, 128), BF16),
        vmem((2, TN, PIECE, 128), BF16),
        vmem((YN, ROWS, WIDE), BF16),
        vmem((FIELDS, 4, ROWS, WIDE), BF16),
        vmem((FIELDS, ROWS, WIDE), BF16),
        vmem((FIELDS, 4, ROWS, WIDE), BF16),
        vmem((S * ROWS, WIDE), BF16),
        vmem((FIELDS, S, ROWS, LON), F32),
        vmem((FIELDS, LAT + 8, WIDE), F32),
        vmem((LAT, WIDE), F32),
        vmem((2, LAT, 128), F32),
        vmem((LAT, LAT), BF16),
        vmem((LAT, LAT), BF16),
        vmem((LAT, LAT), BF16),
        vmem((S * COLS, WIDE), BF16),
        vmem((TN * PIECE, 3 * ROWS), BF16),
        vmem((3 * ROWS, TN * PIECE), BF16),
        vmem((CH, 128), F32),
        vmem((2, PIECE, 128), F32),
        vmem((S, 8, 256), F32),
        vmem((S, 8, 256), F32),
        vmem((OWN, 8, 256), F32),
        dma((8,)), dma((S,)), dma((FIELDS,)),
        dma((2, 4)), dma((2, 4)), dma((4,)), dma((4,)),
        dma((2, YN - 1)), dma((2, YN - 1)), dma((2, TN - 1)), dma((2, TN - 1)),
        dma((TN - 1,)), dma((TN - 1,)), dma((YN - 1,)), dma((YN - 1,)),
        dma((FIELDS, 4)), dma((FIELDS, 4)),
    ]
    in_hbm = pl.BlockSpec(memory_space=pl.ANY)
    in_vmem = pl.BlockSpec(memory_space=pltpu.VMEM)
    return pl.pallas_call(
        kernel,
        out_shape=(jax.ShapeDtypeStruct((MEMB, S, ROWS, LON), F32), jax.ShapeDtypeStruct((S, ROWS, LON), F32)),
        in_specs=[in_hbm] * len(inputs) + [in_vmem, in_vmem],
        out_specs=(in_hbm, in_hbm),
        scratch_shapes=scratch,
        compiler_params=pltpu.CompilerParams(collective_id=0, has_side_effects=True, vmem_limit_bytes=60 << 20),
        name="hessian",
    )(*inputs, channel_error.reshape(1, CH), member_weight.reshape(1, -1))


def solution(mesh):
    in_specs = (
        P("mem", None, "band", None),
        P(None, "band", None),
        P("mem", None, None, "band"),
        P(None, None, "band"),
        P(),
        P(),
        P(None, None, "mem", "band"),
        P("mem", "band"),
        P(None, "mem", "band"),
        P(),
        P(),
    )
    out_specs = (P("mem", None, "band", None), P(None, "band", None))
    return jax.shard_map(shards, mesh=mesh, in_specs=in_specs, out_specs=out_specs, check_vma=False)
```

time: 91.4 us -> 73.6 us (0.81)
  the two profiles are of different devices: /device:TPU:37 before, /device:TPU:1 now
where the time goes in v2:
time: 73.6 us; the launch traced here: 73.5 us
  Pallas kernels  68.8 us (93%)
  local copies, waits for them, and re-layouts  4.01 us (5%)
    pallas_call x1, Pallas kernels, shards(): pl.pallas_call(kernel, out_shape=(jax.ShapeDtypeStruct((MEMB, S, ROWS, LO...  68.8 us
    unnamed x4, local copies, waits for them, and re-layouts  4.01 us

profile of v2, /device:TPU:1, one launch (start us, length us, event | category | flops | bytes accessed | tf_op | source)
XLA Modules:
  0.0 73.5 jit_solution(15300559673365351361)
XLA Ops:
  0.6 68.8 %hessian.1 = (f32[2,4,80,720]{3,2,1,0:T(8,128)}, f32[4,80,720]{2,1,0:T(8,128)}) custom-call(bf16[2,4,80,720]{3,2,1,0:T(8,128)(2,1)} %alpha_hbm.1, bf16[4,80,720]{2,1,0:T(8,128)(2,1)} %static_hbm.1, bf16[2,180,4,320]{3,2,1,0:T(4,128)(2,1)} %bitcast.6, f32[180,4,320]{2,1,0:T(4,128)} %bitcast.7, bf16[720,720]{1,0:T(8,128)(2,1)} %lon_hbm.1, ...), custom_call_target="tpu_custom_call" | custom-call | tf_op jit(solution)/shard_map/hessian/pallas_call | solution.py:414
  69.5 0.0 copy-start
  69.5 3.1 %copy.15 = f32[2,4,80,720]{3,2,1,0:T(8,128)} copy(f32[2,4,80,720]{3,2,1,0:T(8,128)} %get-tuple-element.4) | data formatting | bytes 3686400
  72.5 0.0 copy-done
  72.6 0.9 %copy.16 = f32[4,80,720]{2,1,0:T(8,128)} copy(f32[4,80,720]{2,1,0:T(8,128)S(1)} %copy-done) | data formatting | bytes 1843200
Async XLA Ops:
  69.5 3.1 %copy-start = (f32[4,80,720]{2,1,0:T(8,128)S(1)}, f32[4,80,720]{2,1,0:T(8,128)}, u32[]{:S(2)}) copy-start(f32[4,80,720]{2,1,0:T(8,128)} %get-tuple-element.5) | copy-start | bytes 2764804

commit v3 on v2

v3 whole, which is shorter than its diff:
```python
import functools

import jax
import jax.numpy as jnp
from jax import lax
from jax.experimental import pallas as pl
from jax.experimental.pallas import tpu as pltpu
from jax.sharding import PartitionSpec as P

MESH = pl.DeviceIdType.MESH
F32, BF16, I32 = jnp.float32, jnp.bfloat16, jnp.int32

S, CH, MEMB, FIELDS = 4, 32, 2, 3
ROWS, LAT, LON, COLS = 80, 320, 720, 180
REM = COLS - 128
YN, TN, OWN = 4, 16, 5
WIDE = 768
CHUNKS = 2
TILES = (2, 4)
BASE = (512, 0)
PIECE = (16, 32)
SPAN = ((128, COLS), (0, 128))


def iota(shape, dim):
    return lax.broadcasted_iota(I32, shape, dim)


def one_hot(rows, columns, column_of_row):
    return jnp.where(iota((rows, columns), 1) == column_of_row(iota((rows, columns), 0)), 1.0, 0.0).astype(BF16)


def fifth(x):
    return (x * 205) // 1024


def grid_row(p):
    y = p // ROWS
    t = fifth(p - ROWS * y)
    return OWN * (8 * (t // 2) + 4 * (t % 2) + y) + p - ROWS * y - OWN * t


def packed_lane(row):
    j, s = row // 4, row % 4
    return jnp.where(j < 128, 128 * s + j, 512 + 128 * (s // 2) + 64 * (s % 2) + j - 128)


def piece_row(c, a):
    t, r = a // PIECE[c], a % PIECE[c]
    tile = fifth(r)
    return jnp.where(r < TILES[c] * OWN, ROWS * tile + OWN * t + r - OWN * tile, -1)


def low_half(shape):
    return iota(shape, len(shape) - 1) < 64


def joined(even, odd):
    return jnp.where(low_half(even.shape), even, pltpu.roll(odd, 64, 1))


def joined_high(even, odd):
    return jnp.where(low_half(even.shape), pltpu.roll(even, 64, 1), odd)


def dot(a, b, contract=(1, 0)):
    return lax.dot_general(a, b, (((contract[0],), (contract[1],)), ((), ())), preferred_element_type=F32)


def kernel(
    alpha_hbm, static_hbm, pert_hbm, std_hbm, lon_hbm, lat_hbm, jac_hbm, count_hbm, mask_hbm, error_ref, weight_ref,
    ga_hbm, gs_hbm,
    alpha, static, pert, std, lon, lat, jac, count, mask,
    w, ss, sr, out, spread, rem, order, latp, latpt, spreader, squares, incs, gr,
    fs0, fs1, rl0, rl1, xr0, xr1, rs0, rs1, r10, r11, s20, s21, r20, r21, terms0, terms1, gp0, gp1, gz0, gz1, ag0, ag1,
    bs0, bs1, bl0, bl1, br0, br1, bss0, bss1, brs0, brs1, to0, to1, from0, from1, lhs0, lhs1,
    load_sem, std_sem, store_sem, f_send, f_recv, t_send, t_recv, a_send, a_recv, b_send, b_recv, c_send, c_recv,
    d_send, d_recv, e_send, e_recv, g_send, g_recv,
):
    fs, rl, xr, rs, r1, s2, r2 = (fs0, fs1), (rl0, rl1), (xr0, xr1), (rs0, rs1), (r10, r11), (s20, s21), (r20, r21)
    terms, gp, gz, ag, bs, bl, br = (terms0, terms1), (gp0, gp1), (gz0, gz1), (ag0, ag1), (bs0, bs1), (bl0, bl1), (br0, br1)
    bss, brs, to_piece, from_piece, lhs = (bss0, bss1), (brs0, brs1), (to0, to1), (from0, from1), (lhs0, lhs1)
    lanes = [slice(BASE[c], BASE[c] + 128 * TILES[c]) for c in range(CHUNKS)]

    mem, band = lax.axis_index("mem"), lax.axis_index("band")
    z, x, y = mem // 8, (mem // 4) % 2, mem % 4
    t = 2 * z + x
    chip, core = band // 2, band % 2
    sib, far, cross = 2 * chip + 1 - core, 2 * (1 - chip) + core, 3 - band

    def at_band(b):
        return {"mem": mem, "band": b}

    ys = [lax.rem(y + k, YN) for k in range(1, YN)]
    to_y = [{"mem": 8 * z + 4 * x + v, "band": band} for v in ys]
    ts = [lax.rem(t + k, TN) for k in range(1, TN)]
    to_t = [{"mem": 8 * (v // 2) + 4 * (v % 2) + y, "band": band} for v in ts]

    staged = [(lon_hbm, lon), (alpha_hbm, alpha), (static_hbm, static), (lat_hbm, lat),
              (pert_hbm.reshape(MEMB, S * COLS, LAT), pert), (jac_hbm, jac), (count_hbm, count), (mask_hbm, mask)]
    loads = [pltpu.make_async_copy(src, dst, load_sem.at[i]) for i, (src, dst) in enumerate(staged)]
    loads += [pltpu.make_async_copy(std_hbm.at[:, s, :], std.at[s], std_sem.at[s]) for s in range(S)]
    for load in loads:
        load.start()

    barrier = pltpu.get_barrier_semaphore()
    partners = [at_band(far), at_band(cross)] + to_t + to_y + [at_band(sib)]
    for device in partners:
        pl.semaphore_signal(barrier, inc=1, device_id=device, device_id_type=MESH)

    def remote(src, dst, send, recv, device):
        return pltpu.make_async_remote_copy(
            src_ref=src, dst_ref=dst, send_sem=send, recv_sem=recv, device_id=device, device_id_type=MESH)

    sent = []

    loads[0].wait()
    for b in range(4):
        w[:, 512 + 64 * b : 512 + 64 * b + REM] = lon[:, COLS * b + 128 : COLS * b + COLS]
        w[:, 512 + 64 * b + REM : 576 + 64 * b] = jnp.zeros((LON, 64 - REM), BF16)
        w[:, 128 * b : 128 * b + 128] = lon[:, COLS * b : COLS * b + 128]

    forward = []
    loads[1].wait()
    for c in range(CHUNKS):
        v = dot(alpha[...].reshape(MEMB * S * ROWS, LON), w[:, lanes[c]])
        v = v.reshape(MEMB, S, ROWS, 128 * TILES[c])
        for m in range(MEMB):
            for b in range(4):
                if c == 0:
                    tile = 128 * (b // 2)
                    join = joined if b % 2 == 0 else joined_high
                    for h in range(2):
                        pair = join(v[m, 2 * h][:, tile : tile + 128], v[m, 2 * h + 1][:, tile : tile + 128])
                        fs[c][b, m, :, 128 * h : 128 * h + 128] = pair.astype(BF16)
                else:
                    for s in range(S):
                        fs[c][b, m, :, 128 * s : 128 * s + 128] = v[m, s][:, 128 * b : 128 * b + 128].astype(BF16)
        copies = [
            remote(fs[c].at[far], xr[c].at[band], f_send.at[c, 0], f_recv.at[c, 0], at_band(far)),
            remote(fs[c].at[cross], rl[c], f_send.at[c, 1], f_recv.at[c, 1], at_band(sib)),
            remote(fs[c].at[sib], xr[c].at[band], f_send.at[c, 2], f_recv.at[c, 2], at_band(sib)),
            remote(rl[c], xr[c].at[sib], f_send.at[c, 3], f_recv.at[c, 3], at_band(far)),
        ]
        if c == 0:
            pl.semaphore_wait(barrier, len(partners))
        else:
            forward[0][1].wait_recv()
            forward[0][3].start()
        for copy in copies[:3]:
            copy.start()
        forward.append(copies)
        xr[c][band] = fs[c][band]

    loads[2].wait()
    loads[3].wait()
    v = dot(static[...].reshape(S * ROWS, LON), w[...]).astype(BF16)
    forward[1][1].wait_recv()
    forward[1][3].start()
    own_rows = dot(one_hot(16, LAT, lambda k: jnp.where(k < OWN, OWN * mem + k, -1)), lat[...]).astype(BF16)
    here = jnp.where(iota((LAT, ROWS), 0) == ROWS * band + iota((LAT, ROWS), 1), 1.0, 0.0).astype(BF16)
    own_part = dot(own_rows, here).astype(BF16)
    parts = [dot(own_part, v[ROWS * s : ROWS * s + ROWS])[0:8] for s in range(S)]
    for b in range(4):
        tile = 512 + 128 * (b // 2)
        join = joined if b % 2 == 0 else joined_high
        for s in range(S):
            ss[b, :, 128 * s : 128 * s + 128] = parts[s][:, 128 * b : 128 * b + 128]
        for h in range(2):
            ss[b, :, 512 + 128 * h : 640 + 128 * h] = join(
                parts[2 * h][:, tile : tile + 128], parts[2 * h + 1][:, tile : tile + 128])
    others = (far, cross, sib)
    static_copies = [remote(ss.at[b], sr.at[band], t_send.at[k], t_recv.at[k], at_band(b)) for k, b in enumerate(others)]
    for copy in static_copies:
        copy.start()
    sr[band] = ss[band]

    order[...] = one_hot(LAT, LAT, grid_row)
    latp[...] = dot(order[...], lat[...]).astype(BF16)
    spreader[...] = one_hot(S * COLS, WIDE, packed_lane)
    weights = weight_ref[...].astype(F32)
    coef = weights / jnp.sqrt(jnp.sum(weights * weights, axis=1, keepdims=True))
    loads[4].wait()
    for m in range(MEMB):
        factor = 0.8 * jnp.sum(jnp.where(iota(coef.shape, 1) == MEMB * mem + m, coef, 0.0), axis=1, keepdims=True)
        ordered = dot(order[...], pert[m], (1, 1)).astype(BF16)
        spread[m, 0:LAT] = factor * dot(ordered, spreader[...])
    for c in range(CHUNKS):
        rows, height = TN * PIECE[c], ROWS * TILES[c]
        to_piece[c][...] = one_hot(rows, height, lambda a: piece_row(c, a))

    def sum_first(c):
        for k in (0, 2, 3):
            forward[c][k].wait_recv()
        total = None
        for m in range(MEMB):
            field = dot(latp[...], xr[c][:, m].reshape(LAT, 128 * TILES[c]))
            term = spread[m, 0:LAT, lanes[c]] * field
            total = term if total is None else total + term
        rs[c][...] = total.astype(BF16).reshape(YN, ROWS, 128 * TILES[c])
        copies = [
            remote(rs[c].at[ys[k]], r1[c].at[k], a_send.at[c, k], a_recv.at[c, k], to_y[k]) for k in range(YN - 1)]
        for copy in copies:
            copy.start()
        sent.extend(forward[c])
        return copies

    def sum_second(c, first):
        for copy in first:
            copy.wait_recv()
        total = rs[c][y].astype(F32)
        for k in range(YN - 1):
            total = total + r1[c][k].astype(F32)
        total = total.astype(BF16)
        tall = jnp.concatenate([total[:, 128 * l : 128 * l + 128] for l in range(TILES[c])], axis=0)
        s2[c][...] = dot(to_piece[c][...], tall).astype(BF16).reshape(TN, PIECE[c], 128)
        copies = [
            remote(s2[c].at[ts[k]], r2[c].at[k], b_send.at[c, k], b_recv.at[c, k], to_t[k]) for k in range(TN - 1)]
        for copy in copies:
            copy.start()
        sent.extend(first)
        return copies

    def pixels(c, second):
        for copy in second:
            copy.wait_recv()
        sent.extend(second)
        total = terms[c][...] + s2[c][t].astype(F32)
        for k in range(TN - 1):
            total = total + r2[c][k].astype(F32)
        lo, hi = SPAN[c]
        turned = pltpu.roll(total, 64, 1) if c == 0 else None
        for i in range(OWN):
            for s in range(S):
                row = OWN * s + i if c else OWN * (s // 2) + i
                source = total if c or s % 2 == 0 else turned
                incs[i, s : s + 1, :] = source[row : row + 1, :]
        inc = [incs[i, 0:S, 0 : hi - lo] for i in range(OWN)]
        counts = count[:, lo:hi].astype(F32)

        def channels(step, grads):
            base = pl.multiple_of(8 * step, 8)
            square = squares[pl.ds(base, 8), 0:1]
            grads = list(grads)
            for i in range(OWN):
                weight = mask[i, pl.ds(base, 8), lo:hi].astype(F32) * counts[i : i + 1, :] / square
                for n in range(8):
                    jac_n = jac[base + n, i, :, lo:hi].astype(F32)
                    radiance = jnp.sum(jac_n * inc[i], axis=0, keepdims=True)
                    grads[i] = grads[i] + jac_n * (weight[n : n + 1, :] * radiance)
            return tuple(grads)

        grads = lax.fori_loop(0, CH // 8, channels, tuple(jnp.zeros((S, hi - lo), F32) for _ in range(OWN)))
        gr[...] = jnp.zeros_like(gr)
        for i in range(OWN):
            for s in range(S):
                row = OWN * s + i if c else OWN * (s // 2) + i
                half = 0 if c else s % 2
                gr[half, row : row + 1, 0 : hi - lo] = grads[i][s : s + 1, :].astype(BF16).astype(F32)
        gp[c][...] = (gr[0] if c else joined(gr[0, 0 : PIECE[0]], gr[1, 0 : PIECE[0]])).astype(BF16)
        copies = [remote(gp[c], gz[c].at[t], c_send.at[c, k], c_recv.at[c, k], to_t[k]) for k in range(TN - 1)]
        for copy in copies:
            copy.start()
        gz[c][t] = gp[c][...]
        return copies

    def gather(c, third):
        for copy in third:
            copy.wait_recv()
        sent.extend(third)
        tall = dot(from_piece[c][...], gz[c][...].reshape(TN * PIECE[c], 128)).astype(BF16)
        for l in range(TILES[c]):
            ag[c][y, :, 128 * l : 128 * l + 128] = tall[ROWS * l : ROWS * l + ROWS]
        copies = [remote(ag[c].at[y], ag[c].at[y], d_send.at[c, k], d_recv.at[c, k], to_y[k]) for k in range(YN - 1)]
        for copy in copies:
            copy.start()
        return copies

    source, half = far + (cross - far) * (y // 2), y % 2

    def adjoint(c, fourth):
        for copy in fourth:
            copy.wait_recv()
        sent.extend(fourth)
        gradient = ag[c][...].reshape(LAT, 128 * TILES[c]).astype(F32)
        width = 64 * TILES[c]
        back = dot(latpt[...], (spread[MEMB, 0:LAT, lanes[c]] * gradient).astype(BF16)).astype(BF16)
        back = back.reshape(4, ROWS, 128 * TILES[c])
        for h in range(2):
            bss[c][h] = back[:, :, width * h : width * h + width]
        fixed = [
            remote(bss[c].at[half, source], brs[c].at[half, band], g_send.at[c, 0], g_recv.at[c, 0], at_band(source)),
            remote(bss[c].at[:, sib], brs[c].at[:, band], g_send.at[c, 1], g_recv.at[c, 1], at_band(sib)),
        ] + [
            remote(brs[c].at[half, source], brs[c].at[half, source], g_send.at[c, 2 + k], g_recv.at[c, 2 + k], to_y[k])
            for k in range(YN - 1)]
        for copy in fixed[:2]:
            copy.start()
        for m in range(MEMB):
            back = dot(latpt[...], (spread[m, 0:LAT, lanes[c]] * gradient).astype(BF16)).astype(BF16)
            bs[c][:, m] = back.reshape(4, ROWS, 128 * TILES[c])
        copies = [
            remote(bs[c].at[far], br[c].at[band], e_send.at[c, 0], e_recv.at[c, 0], at_band(far)),
            remote(bs[c].at[cross], bl[c], e_send.at[c, 1], e_recv.at[c, 1], at_band(sib)),
            remote(bs[c].at[sib], br[c].at[band], e_send.at[c, 2], e_recv.at[c, 2], at_band(sib)),
            remote(bl[c], br[c].at[sib], e_send.at[c, 3], e_recv.at[c, 3], at_band(far)),
        ]
        for copy in copies[:3]:
            copy.start()
        br[c][band] = bs[c][band]
        for h in range(2):
            brs[c][h, band] = bss[c][h, band]
        return copies, fixed

    def pass_on(c, copies, fixed):
        copies[1].wait_recv()
        copies[3].start()
        fixed[0].wait_recv()
        for copy in fixed[2:]:
            copy.start()

    first = [sum_first(0)]

    for load in loads[8:]:
        load.wait()
    rem[...] = jnp.zeros_like(rem)
    for h in range(2):
        for s in range(2):
            value = std[2 * h + s]
            ordered = None
            for _ in range(3):
                top = value.astype(BF16)
                term = dot(order[...], top, (1, 1))
                ordered = term if ordered is None else ordered + term
                value = value - top.astype(F32)
            ordered = 0.6 * ordered
            spread[MEMB, 0:LAT, 128 * (2 * h + s) : 128 * (2 * h + s) + 128] = ordered[:, 0:128]
            rem[s, :, 0:REM] = ordered[:, 128:COLS]
        spread[MEMB, 0:LAT, 512 + 128 * h : 640 + 128 * h] = joined(rem[0], rem[1])

    first.append(sum_first(1))
    spread[:, LAT:] = jnp.zeros((FIELDS, 8, WIDE), F32)
    first_row = ROWS * y + OWN * t
    shift = first_row % 8
    own_std = spread[MEMB, pl.ds(pl.multiple_of(first_row - shift, 8), 16), :]
    own_std = pltpu.roll(own_std, (16 - shift) % 16, 0)[0:8]
    for copy in static_copies:
        copy.wait_recv()
    sent.extend(static_copies)
    static_term = own_std * (sr[0] + sr[1] + sr[2] + sr[3])
    for c in range(CHUNKS):
        terms[c][...] = jnp.zeros_like(terms[c])
        for l in range(TILES[c]):
            terms[c][OWN * l : OWN * l + OWN] = static_term[0:OWN, BASE[c] + 128 * l : BASE[c] + 128 * l + 128]

    second = [sum_second(0, first[0])]
    latpt[...] = dot(jnp.transpose(lat[...].astype(F32)).astype(BF16), order[...], (1, 1)).astype(BF16)
    for c in range(CHUNKS):
        rows, height = TN * PIECE[c], ROWS * TILES[c]
        hot = iota((height, rows), 0) == piece_row(c, iota((height, rows), 1))
        from_piece[c][...] = jnp.where(hot, 1.0, 0.0).astype(BF16)
    error = jnp.sum(jnp.where(iota((CH, CH), 0) == iota((CH, CH), 1), error_ref[...], 0.0), axis=1, keepdims=True)
    squares[...] = jnp.broadcast_to(error * error, squares.shape)
    for load in loads[5:8]:
        load.wait()

    second.append(sum_second(1, first[1]))

    third = [pixels(0, second[0])]

    third.append(pixels(1, second[1]))

    fourth = [gather(0, third[0])]

    fourth.append(gather(1, third[1]))

    ways = [adjoint(0, fourth[0])]
    pass_on(0, *ways[0])

    ways.append(adjoint(1, fourth[1]))

    copies, fixed = ways[0]
    for copy in copies[:1] + copies[2:] + fixed[1:]:
        copy.wait_recv()
    for f in range(FIELDS):
        for h in range(2):
            if f < MEMB:
                tiles = [br[0][b, f, :, 128 * h : 128 * h + 128].astype(F32) for b in range(4)]
            else:
                tiles = [brs[0][h, b].astype(F32) for b in range(4)]
            for s in range(2):
                join = joined if s == 0 else joined_high
                for g in range(2):
                    pair = join(tiles[2 * g], tiles[2 * g + 1]).astype(BF16)
                    lhs[0][pl.ds((2 * h + s) * ROWS, ROWS), 128 * g : 128 * g + 128] = pair
        base = alpha[f] if f < MEMB else static[...]
        out[f] = base.astype(F32) + dot(lhs[0][...], w[:, lanes[0]], (1, 1)).reshape(S, ROWS, LON)
        if f == 0:
            ways[1][0][1].wait_recv()
            ways[1][0][3].start()
    ways[1][1][0].wait_recv()
    for copy in ways[1][1][2:]:
        copy.start()

    stores = []
    copies, fixed = ways[1]
    for f in range(FIELDS):
        if f == 0:
            for copy in copies[:1] + copies[2:]:
                copy.wait_recv()
        if f == MEMB:
            for copy in fixed[1:]:
                copy.wait_recv()
        for s in range(S):
            for b in range(4):
                if f < MEMB:
                    tile = br[1][b, f, :, 128 * s : 128 * s + 128]
                else:
                    tile = brs[1][s // 2, b, :, 128 * (s % 2) : 128 * (s % 2) + 128]
                lhs[1][ROWS * s : ROWS * s + ROWS, 128 * b : 128 * b + 128] = tile
        out[f] = out[f] + dot(lhs[1][...], w[:, lanes[1]], (1, 1)).reshape(S, ROWS, LON)
        store = pltpu.make_async_copy(out.at[f], ga_hbm.at[f] if f < MEMB else gs_hbm, store_sem.at[f])
        store.start()
        stores.append(store)
    for copies, fixed in ways:
        sent.extend(copies)
        sent.extend(fixed)
    for store in stores:
        store.wait()
    for copy in sent:
        copy.wait_send()


def shards(alpha, static_ctl, perturbations, static_std, lon_root, lat_root, jacobian, obs_count, channel_mask,
           channel_error, member_weight):
    inputs = [alpha, static_ctl, jnp.transpose(perturbations, (0, 3, 1, 2)), jnp.transpose(static_std, (2, 0, 1)),
              lon_root, lat_root, jnp.transpose(jacobian, (0, 2, 1, 3)), obs_count, jnp.transpose(channel_mask, (1, 0, 2))]
    dma, vmem = pltpu.SemaphoreType.DMA, pltpu.VMEM
    scratch = [
        vmem((MEMB, S, ROWS, LON), BF16),
        vmem((S, ROWS, LON), BF16),
        vmem((MEMB, S * COLS, LAT), BF16),
        vmem((S, COLS, LAT), F32),
        vmem((LON, LON), BF16),
        vmem((LAT, LAT), BF16),
        vmem((CH, OWN, S, COLS), BF16),
        vmem((OWN, COLS), I32),
        vmem((OWN, CH, COLS), I32),
        vmem((LON, WIDE), BF16),
        vmem((4, 8, WIDE), F32),
        vmem((4, 8, WIDE), F32),
        vmem((FIELDS, S, ROWS, LON), F32),
        vmem((FIELDS, LAT + 8, WIDE), F32),
        vmem((2, LAT, 128), F32),
        vmem((LAT, LAT), BF16),
        vmem((LAT, LAT), BF16),
        vmem((LAT, LAT), BF16),
        vmem((S * COLS, WIDE), BF16),
        vmem((CH, 128), F32),
        vmem((OWN, 8, 128), F32),
        vmem((2, 32, 128), F32),
    ]

    def both(shape, kind):
        return [vmem(shape(128 * TILES[c], PIECE[c], ROWS * TILES[c]), kind) for c in range(CHUNKS)]

    scratch += both(lambda n, r, h: (4, MEMB, ROWS, n), BF16)
    scratch += both(lambda n, r, h: (MEMB, ROWS, n), BF16)
    scratch += both(lambda n, r, h: (4, MEMB, ROWS, n), BF16)
    scratch += both(lambda n, r, h: (YN, ROWS, n), BF16)
    scratch += both(lambda n, r, h: (YN - 1, ROWS, n), BF16)
    scratch += both(lambda n, r, h: (TN, r, 128), BF16)
    scratch += both(lambda n, r, h: (TN - 1, r, 128), BF16)
    scratch += both(lambda n, r, h: (r, 128), F32)
    scratch += both(lambda n, r, h: (r, 128), BF16)
    scratch += both(lambda n, r, h: (TN, r, 128), BF16)
    scratch += both(lambda n, r, h: (YN, ROWS, n), BF16)
    scratch += both(lambda n, r, h: (4, MEMB, ROWS, n), BF16)
    scratch += both(lambda n, r, h: (MEMB, ROWS, n), BF16)
    scratch += both(lambda n, r, h: (4, MEMB, ROWS, n), BF16)
    scratch += both(lambda n, r, h: (2, 4, ROWS, n // 2), BF16)
    scratch += both(lambda n, r, h: (2, 4, ROWS, n // 2), BF16)
    scratch += both(lambda n, r, h: (TN * r, h), BF16)
    scratch += both(lambda n, r, h: (h, TN * r), BF16)
    scratch += both(lambda n, r, h: (S * ROWS, n), BF16)
    scratch += [
        dma((8,)), dma((S,)), dma((FIELDS,)),
        dma((2, 4)), dma((2, 4)), dma((3,)), dma((3,)),
        dma((2, YN - 1)), dma((2, YN - 1)), dma((2, TN - 1)), dma((2, TN - 1)),
        dma((2, TN - 1)), dma((2, TN - 1)), dma((2, YN - 1)), dma((2, YN - 1)),
        dma((2, 4)), dma((2, 4)), dma((2, YN + 1)), dma((2, YN + 1)),
    ]
    in_hbm = pl.BlockSpec(memory_space=pl.ANY)
    in_vmem = pl.BlockSpec(memory_space=pltpu.VMEM)
    return pl.pallas_call(
        kernel,
        out_shape=(jax.ShapeDtypeStruct((MEMB, S, ROWS, LON), F32), jax.ShapeDtypeStruct((S, ROWS, LON), F32)),
        in_specs=[in_hbm] * len(inputs) + [in_vmem, in_vmem],
        out_specs=(in_hbm, in_hbm),
        scratch_shapes=scratch,
        compiler_params=pltpu.CompilerParams(collective_id=0, has_side_effects=True, vmem_limit_bytes=60 << 20),
        name="hessian",
    )(*inputs, channel_error.reshape(1, CH), member_weight.reshape(1, -1))


def solution(mesh):
    in_specs = (
        P("mem", None, "band", None),
        P(None, "band", None),
        P("mem", None, None, "band"),
        P(None, None, "band"),
        P(),
        P(),
        P(None, None, "mem", "band"),
        P("mem", "band"),
        P(None, "mem", "band"),
        P(),
        P(),
    )
    out_specs = (P("mem", None, "band", None), P(None, "band", None))
    return jax.shard_map(shards, mesh=mesh, in_specs=in_specs, out_specs=out_specs, check_vma=False)
```

time: 73.6 us -> 66.9 us (0.909)
  Pallas kernels: 68.8 us -> 62.1 us
    pallas_call x1, Pallas kernels: 68.8 us -> 62.1 us  [shards(): pl.pallas_call(kernel, out_shape=(jax.ShapeDtypeStruct((MEMB, S, ROWS, LO...]
where the time goes in v3:
time: 66.9 us; the launch traced here: 66.8 us
  Pallas kernels  62.1 us (93%)
  local copies, waits for them, and re-layouts  4.01 us (6%)
    pallas_call x1, Pallas kernels, shards(): pl.pallas_call(kernel, out_shape=(jax.ShapeDtypeStruct((MEMB, S, ROWS, LO...  62.1 us
    unnamed x4, local copies, waits for them, and re-layouts  4.01 us

profile of v3, /device:TPU:1, one launch (start us, length us, event | category | flops | bytes accessed | tf_op | source)
XLA Modules:
  0.0 66.8 jit_solution(17648305610780097972)
XLA Ops:
  0.6 62.1 %hessian.1 = (f32[2,4,80,720]{3,2,1,0:T(8,128)}, f32[4,80,720]{2,1,0:T(8,128)}) custom-call(bf16[2,4,80,720]{3,2,1,0:T(8,128)(2,1)} %alpha_hbm.1, bf16[4,80,720]{2,1,0:T(8,128)(2,1)} %static_hbm.1, bf16[2,180,4,320]{3,2,1,0:T(4,128)(2,1)} %bitcast.6, f32[180,4,320]{2,1,0:T(4,128)} %bitcast.7, bf16[720,720]{1,0:T(8,128)(2,1)} %lon_hbm.1, ...), custom_call_target="tpu_custom_call" | custom-call | tf_op jit(solution)/shard_map/hessian/pallas_call | solution.py:495
  62.7 0.0 copy-start
  62.8 3.1 %copy.15 = f32[2,4,80,720]{3,2,1,0:T(8,128)} copy(f32[2,4,80,720]{3,2,1,0:T(8,128)} %get-tuple-element.4) | data formatting | bytes 3686400
  65.8 0.0 copy-done
  65.8 0.9 %copy.16 = f32[4,80,720]{2,1,0:T(8,128)} copy(f32[4,80,720]{2,1,0:T(8,128)S(1)} %copy-done) | data formatting | bytes 1843200
Async XLA Ops:
  62.7 3.1 %copy-start = (f32[4,80,720]{2,1,0:T(8,128)S(1)}, f32[4,80,720]{2,1,0:T(8,128)}, u32[]{:S(2)}) copy-start(f32[4,80,720]{2,1,0:T(8,128)} %get-tuple-element.5) | copy-start | bytes 2764804

commit v4 on v3

--- a/solution.py
+++ b/solution.py
@@ -10,7 +10,7 @@
 MESH = pl.DeviceIdType.MESH
 F32, BF16, I32 = jnp.float32, jnp.bfloat16, jnp.int32
 
-S, CH, MEMB, FIELDS = 4, 32, 2, 3
+S, CH, MEM, MEMB, FIELDS = 4, 32, 128, 2, 3
 ROWS, LAT, LON, COLS = 80, 320, 720, 180
 REM = COLS - 128
 YN, TN, OWN = 4, 16, 5
@@ -18,8 +18,7 @@
 CHUNKS = 2
 TILES = (2, 4)
 BASE = (512, 0)
-PIECE = (16, 32)
-SPAN = ((128, COLS), (0, 128))
+PIECE, ALL = 32, 6
 
 
 def iota(shape, dim):
@@ -45,10 +44,10 @@
     return jnp.where(j < 128, 128 * s + j, 512 + 128 * (s // 2) + 64 * (s % 2) + j - 128)
 
 
-def piece_row(c, a):
-    t, r = a // PIECE[c], a % PIECE[c]
+def piece_row(a):
+    t, r = a // PIECE, a % PIECE
     tile = fifth(r)
-    return jnp.where(r < TILES[c] * OWN, ROWS * tile + OWN * t + r - OWN * tile, -1)
+    return jnp.where(r < ALL * OWN, ROWS * tile + OWN * t + r - OWN * tile, -1)
 
 
 def low_half(shape):
@@ -68,18 +67,18 @@
 
 
 def kernel(
-    alpha_hbm, static_hbm, pert_hbm, std_hbm, lon_hbm, lat_hbm, jac_hbm, count_hbm, mask_hbm, error_ref, weight_ref,
+    alpha_hbm, static_hbm, pert_hbm, std_hbm, lon_hbm, lat_hbm, jac_hbm, count_hbm, mask_hbm, error_hbm, weight_hbm,
     ga_hbm, gs_hbm,
-    alpha, static, pert, std, lon, lat, jac, count, mask,
-    w, ss, sr, out, spread, rem, order, latp, latpt, spreader, squares, incs, gr,
-    fs0, fs1, rl0, rl1, xr0, xr1, rs0, rs1, r10, r11, s20, s21, r20, r21, terms0, terms1, gp0, gp1, gz0, gz1, ag0, ag1,
-    bs0, bs1, bl0, bl1, br0, br1, bss0, bss1, brs0, brs1, to0, to1, from0, from1, lhs0, lhs1,
+    alpha, static, pert, std, lon, lat, jac, count, mask, error_row, weight_row,
+    w, ss, sr, out, spread, rem, order, latp, latpt, spreader, squares, incs, isc, gsc, s2, r2, terms, gp, gz, to_piece,
+    from_piece,
+    fs0, fs1, rl0, rl1, xr0, xr1, rs0, rs1, r10, r11, ag0, ag1,
+    bs0, bs1, bl0, bl1, br0, br1, bss0, bss1, brs0, brs1, lhs0, lhs1,
     load_sem, std_sem, store_sem, f_send, f_recv, t_send, t_recv, a_send, a_recv, b_send, b_recv, c_send, c_recv,
     d_send, d_recv, e_send, e_recv, g_send, g_recv,
 ):
-    fs, rl, xr, rs, r1, s2, r2 = (fs0, fs1), (rl0, rl1), (xr0, xr1), (rs0, rs1), (r10, r11), (s20, s21), (r20, r21)
-    terms, gp, gz, ag, bs, bl, br = (terms0, terms1), (gp0, gp1), (gz0, gz1), (ag0, ag1), (bs0, bs1), (bl0, bl1), (br0, br1)
-    bss, brs, to_piece, from_piece, lhs = (bss0, bss1), (brs0, brs1), (to0, to1), (from0, from1), (lhs0, lhs1)
+    fs, rl, xr, rs, r1, ag = (fs0, fs1), (rl0, rl1), (xr0, xr1), (rs0, rs1), (r10, r11), (ag0, ag1)
+    bs, bl, br, bss, brs, lhs = (bs0, bs1), (bl0, bl1), (br0, br1), (bss0, bss1), (brs0, brs1), (lhs0, lhs1)
     lanes = [slice(BASE[c], BASE[c] + 128 * TILES[c]) for c in range(CHUNKS)]
 
     mem, band = lax.axis_index("mem"), lax.axis_index("band")
@@ -97,7 +96,8 @@
     to_t = [{"mem": 8 * (v // 2) + 4 * (v % 2) + y, "band": band} for v in ts]
 
     staged = [(lon_hbm, lon), (alpha_hbm, alpha), (static_hbm, static), (lat_hbm, lat),
-              (pert_hbm.reshape(MEMB, S * COLS, LAT), pert), (jac_hbm, jac), (count_hbm, count), (mask_hbm, mask)]
+              (pert_hbm.reshape(MEMB, S * COLS, LAT), pert), (jac_hbm, jac), (count_hbm, count), (mask_hbm, mask),
+              (error_hbm, error_row), (weight_hbm, weight_row)]
     loads = [pltpu.make_async_copy(src, dst, load_sem.at[i]) for i, (src, dst) in enumerate(staged)]
     loads += [pltpu.make_async_copy(std_hbm.at[:, s, :], std.at[s], std_sem.at[s]) for s in range(S)]
     for load in loads:
@@ -142,21 +142,12 @@
             remote(fs[c].at[sib], xr[c].at[band], f_send.at[c, 2], f_recv.at[c, 2], at_band(sib)),
             remote(rl[c], xr[c].at[sib], f_send.at[c, 3], f_recv.at[c, 3], at_band(far)),
         ]
-        if c == 0:
-            pl.semaphore_wait(barrier, len(partners))
-        else:
-            forward[0][1].wait_recv()
-            forward[0][3].start()
-        for copy in copies[:3]:
-            copy.start()
         forward.append(copies)
         xr[c][band] = fs[c][band]
 
     loads[2].wait()
     loads[3].wait()
     v = dot(static[...].reshape(S * ROWS, LON), w[...]).astype(BF16)
-    forward[1][1].wait_recv()
-    forward[1][3].start()
     own_rows = dot(one_hot(16, LAT, lambda k: jnp.where(k < OWN, OWN * mem + k, -1)), lat[...]).astype(BF16)
     here = jnp.where(iota((LAT, ROWS), 0) == ROWS * band + iota((LAT, ROWS), 1), 1.0, 0.0).astype(BF16)
     own_part = dot(own_rows, here).astype(BF16)
@@ -171,23 +162,30 @@
                 parts[2 * h][:, tile : tile + 128], parts[2 * h + 1][:, tile : tile + 128])
     others = (far, cross, sib)
     static_copies = [remote(ss.at[b], sr.at[band], t_send.at[k], t_recv.at[k], at_band(b)) for k, b in enumerate(others)]
-    for copy in static_copies:
-        copy.start()
     sr[band] = ss[band]
-
     order[...] = one_hot(LAT, LAT, grid_row)
     latp[...] = dot(order[...], lat[...]).astype(BF16)
+    pl.semaphore_wait(barrier, len(partners))
+    for c, k in ((0, 0), (0, 1), (1, 1)):
+        forward[c][k].start()
+    forward[0][1].wait_recv()
+    forward[0][3].start()
+    forward[1][0].start()
+    forward[1][1].wait_recv()
+    forward[1][3].start()
+    for copy in [forward[0][2], forward[1][2]] + static_copies:
+        copy.start()
+
     spreader[...] = one_hot(S * COLS, WIDE, packed_lane)
-    weights = weight_ref[...].astype(F32)
+    loads[9].wait()
+    weights = weight_row[...].astype(F32)
     coef = weights / jnp.sqrt(jnp.sum(weights * weights, axis=1, keepdims=True))
     loads[4].wait()
     for m in range(MEMB):
         factor = 0.8 * jnp.sum(jnp.where(iota(coef.shape, 1) == MEMB * mem + m, coef, 0.0), axis=1, keepdims=True)
         ordered = dot(order[...], pert[m], (1, 1)).astype(BF16)
         spread[m, 0:LAT] = factor * dot(ordered, spreader[...])
-    for c in range(CHUNKS):
-        rows, height = TN * PIECE[c], ROWS * TILES[c]
-        to_piece[c][...] = one_hot(rows, height, lambda a: piece_row(c, a))
+    to_piece[...] = one_hot(TN * PIECE, ALL * ROWS, piece_row)
 
     def sum_first(c):
         for k in (0, 2, 3):
@@ -203,77 +201,6 @@
         for copy in copies:
             copy.start()
         sent.extend(forward[c])
-        return copies
-
-    def sum_second(c, first):
-        for copy in first:
-            copy.wait_recv()
-        total = rs[c][y].astype(F32)
-        for k in range(YN - 1):
-            total = total + r1[c][k].astype(F32)
-        total = total.astype(BF16)
-        tall = jnp.concatenate([total[:, 128 * l : 128 * l + 128] for l in range(TILES[c])], axis=0)
-        s2[c][...] = dot(to_piece[c][...], tall).astype(BF16).reshape(TN, PIECE[c], 128)
-        copies = [
-            remote(s2[c].at[ts[k]], r2[c].at[k], b_send.at[c, k], b_recv.at[c, k], to_t[k]) for k in range(TN - 1)]
-        for copy in copies:
-            copy.start()
-        sent.extend(first)
-        return copies
-
-    def pixels(c, second):
-        for copy in second:
-            copy.wait_recv()
-        sent.extend(second)
-        total = terms[c][...] + s2[c][t].astype(F32)
-        for k in range(TN - 1):
-            total = total + r2[c][k].astype(F32)
-        lo, hi = SPAN[c]
-        turned = pltpu.roll(total, 64, 1) if c == 0 else None
-        for i in range(OWN):
-            for s in range(S):
-                row = OWN * s + i if c else OWN * (s // 2) + i
-                source = total if c or s % 2 == 0 else turned
-                incs[i, s : s + 1, :] = source[row : row + 1, :]
-        inc = [incs[i, 0:S, 0 : hi - lo] for i in range(OWN)]
-        counts = count[:, lo:hi].astype(F32)
-
-        def channels(step, grads):
-            base = pl.multiple_of(8 * step, 8)
-            square = squares[pl.ds(base, 8), 0:1]
-            grads = list(grads)
-            for i in range(OWN):
-                weight = mask[i, pl.ds(base, 8), lo:hi].astype(F32) * counts[i : i + 1, :] / square
-                for n in range(8):
-                    jac_n = jac[base + n, i, :, lo:hi].astype(F32)
-                    radiance = jnp.sum(jac_n * inc[i], axis=0, keepdims=True)
-                    grads[i] = grads[i] + jac_n * (weight[n : n + 1, :] * radiance)
-            return tuple(grads)
-
-        grads = lax.fori_loop(0, CH // 8, channels, tuple(jnp.zeros((S, hi - lo), F32) for _ in range(OWN)))
-        gr[...] = jnp.zeros_like(gr)
-        for i in range(OWN):
-            for s in range(S):
-                row = OWN * s + i if c else OWN * (s // 2) + i
-                half = 0 if c else s % 2
-                gr[half, row : row + 1, 0 : hi - lo] = grads[i][s : s + 1, :].astype(BF16).astype(F32)
-        gp[c][...] = (gr[0] if c else joined(gr[0, 0 : PIECE[0]], gr[1, 0 : PIECE[0]])).astype(BF16)
-        copies = [remote(gp[c], gz[c].at[t], c_send.at[c, k], c_recv.at[c, k], to_t[k]) for k in range(TN - 1)]
-        for copy in copies:
-            copy.start()
-        gz[c][t] = gp[c][...]
-        return copies
-
-    def gather(c, third):
-        for copy in third:
-            copy.wait_recv()
-        sent.extend(third)
-        tall = dot(from_piece[c][...], gz[c][...].reshape(TN * PIECE[c], 128)).astype(BF16)
-        for l in range(TILES[c]):
-            ag[c][y, :, 128 * l : 128 * l + 128] = tall[ROWS * l : ROWS * l + ROWS]
-        copies = [remote(ag[c].at[y], ag[c].at[y], d_send.at[c, k], d_recv.at[c, k], to_y[k]) for k in range(YN - 1)]
-        for copy in copies:
-            copy.start()
         return copies
 
     source, half = far + (cross - far) * (y // 2), y % 2
@@ -321,7 +248,7 @@
 
     first = [sum_first(0)]
 
-    for load in loads[8:]:
+    for load in loads[10:]:
         load.wait()
     rem[...] = jnp.zeros_like(rem)
     for h in range(2):
@@ -348,31 +275,87 @@
         copy.wait_recv()
     sent.extend(static_copies)
     static_term = own_std * (sr[0] + sr[1] + sr[2] + sr[3])
+    terms[...] = jnp.zeros_like(terms)
+    for l in range(ALL):
+        terms[OWN * l : OWN * l + OWN] = static_term[0:OWN, 128 * l : 128 * l + 128]
+
+    tiles = [None] * ALL
     for c in range(CHUNKS):
-        terms[c][...] = jnp.zeros_like(terms[c])
+        for copy in first[c]:
+            copy.wait_recv()
+        sent.extend(first[c])
+        total = rs[c][y].astype(F32)
+        for k in range(YN - 1):
+            total = total + r1[c][k].astype(F32)
         for l in range(TILES[c]):
-            terms[c][OWN * l : OWN * l + OWN] = static_term[0:OWN, BASE[c] + 128 * l : BASE[c] + 128 * l + 128]
-
-    second = [sum_second(0, first[0])]
+            tiles[BASE[c] // 128 + l] = total[:, 128 * l : 128 * l + 128].astype(BF16)
+    s2[...] = dot(to_piece[...], jnp.concatenate(tiles, axis=0)).astype(BF16).reshape(TN, PIECE, 128)
+    second = [remote(s2.at[ts[k]], r2.at[k], b_send.at[k], b_recv.at[k], to_t[k]) for k in range(TN - 1)]
+    for copy in second:
+        copy.start()
     latpt[...] = dot(jnp.transpose(lat[...].astype(F32)).astype(BF16), order[...], (1, 1)).astype(BF16)
+    hot = iota((ALL * ROWS, TN * PIECE), 0) == piece_row(iota((ALL * ROWS, TN * PIECE), 1))
+    from_piece[...] = jnp.where(hot, 1.0, 0.0).astype(BF16)
+    for load in loads[5:9]:
+        load.wait()
+    error = jnp.sum(jnp.where(iota((CH, CH), 0) == iota((CH, CH), 1), error_row[...], 0.0), axis=1, keepdims=True)
+    squares[...] = jnp.broadcast_to(error * error, squares.shape)
+
+    for copy in second:
+        copy.wait_recv()
+    sent.extend(second)
+    total = terms[...] + s2[t].astype(F32)
+    for k in range(TN - 1):
+        total = total + r2[k].astype(F32)
+    turned = pltpu.roll(total, 64, 1)
+    for s in range(S):
+        row = OWN * (4 + s // 2)
+        isc[s, 0:OWN, 0:128] = total[OWN * s : OWN * s + OWN]
+        isc[s, 0:OWN, 128:256] = (total if s % 2 == 0 else turned)[row : row + OWN]
+    for i in range(OWN):
+        for s in range(S):
+            incs[i, s : s + 1, :] = isc[s, i : i + 1, :]
+    inc = [incs[i, 0:S, 0:COLS] for i in range(OWN)]
+    counts = count[...].astype(F32)
+
+    def channels(step, grads):
+        base = pl.multiple_of(8 * step, 8)
+        square = squares[pl.ds(base, 8), 0:1]
+        grads = list(grads)
+        for i in range(OWN):
+            weight = mask[i, pl.ds(base, 8), :].astype(F32) * counts[i : i + 1, :] / square
+            for n in range(8):
+                jac_n = jac[base + n, i].astype(F32)
+                radiance = jnp.sum(jac_n * inc[i], axis=0, keepdims=True)
+                grads[i] = grads[i] + jac_n * (weight[n : n + 1, :] * radiance)
+        return tuple(grads)
+
+    grads = lax.fori_loop(0, CH // 8, channels, tuple(jnp.zeros((S, COLS), F32) for _ in range(OWN)))
+    gsc[...] = jnp.zeros_like(gsc)
+    for i in range(OWN):
+        for s in range(S):
+            gsc[s, i : i + 1, 0:COLS] = grads[i][s : s + 1, :].astype(BF16).astype(F32)
+    piece = [gsc[s, 0:OWN, 0:128] for s in range(S)]
+    piece += [joined(gsc[2 * h, :, 128:256], gsc[2 * h + 1, :, 128:256])[0:OWN] for h in range(2)]
+    gp[...] = jnp.concatenate(piece + [jnp.zeros((PIECE - ALL * OWN, 128), F32)], axis=0).astype(BF16)
+
+    third = [remote(gp, gz.at[t], c_send.at[k], c_recv.at[k], to_t[k]) for k in range(TN - 1)]
+    for copy in third:
+        copy.start()
+    gz[t] = gp[...]
+    for copy in third:
+        copy.wait_recv()
+    sent.extend(third)
+    tall = dot(from_piece[...], gz[...].reshape(TN * PIECE, 128)).astype(BF16)
+    fourth = []
     for c in range(CHUNKS):
-        rows, height = TN * PIECE[c], ROWS * TILES[c]
-        hot = iota((height, rows), 0) == piece_row(c, iota((height, rows), 1))
-        from_piece[c][...] = jnp.where(hot, 1.0, 0.0).astype(BF16)
-    error = jnp.sum(jnp.where(iota((CH, CH), 0) == iota((CH, CH), 1), error_ref[...], 0.0), axis=1, keepdims=True)
-    squares[...] = jnp.broadcast_to(error * error, squares.shape)
-    for load in loads[5:8]:
-        load.wait()
-
-    second.append(sum_second(1, first[1]))
-
-    third = [pixels(0, second[0])]
-
-    third.append(pixels(1, second[1]))
-
-    fourth = [gather(0, third[0])]
-
-    fourth.append(gather(1, third[1]))
+        for l in range(TILES[c]):
+            row = ROWS * (BASE[c] // 128 + l)
+            ag[c][y, :, 128 * l : 128 * l + 128] = tall[row : row + ROWS]
+        copies = [remote(ag[c].at[y], ag[c].at[y], d_send.at[c, k], d_recv.at[c, k], to_y[k]) for k in range(YN - 1)]
+        for copy in copies:
+            copy.start()
+        fourth.append(copies)
 
     ways = [adjoint(0, fourth[0])]
     pass_on(0, *ways[0])
@@ -434,7 +417,8 @@
 def shards(alpha, static_ctl, perturbations, static_std, lon_root, lat_root, jacobian, obs_count, channel_mask,
            channel_error, member_weight):
     inputs = [alpha, static_ctl, jnp.transpose(perturbations, (0, 3, 1, 2)), jnp.transpose(static_std, (2, 0, 1)),
-              lon_root, lat_root, jnp.transpose(jacobian, (0, 2, 1, 3)), obs_count, jnp.transpose(channel_mask, (1, 0, 2))]
+              lon_root, lat_root, jnp.transpose(jacobian, (0, 2, 1, 3)), obs_count, jnp.transpose(channel_mask, (1, 0, 2)),
+              channel_error.reshape(1, CH), member_weight.reshape(1, MEM)]
     dma, vmem = pltpu.SemaphoreType.DMA, pltpu.VMEM
     scratch = [
         vmem((MEMB, S, ROWS, LON), BF16),
@@ -446,6 +430,8 @@
         vmem((CH, OWN, S, COLS), BF16),
         vmem((OWN, COLS), I32),
         vmem((OWN, CH, COLS), I32),
+        vmem((1, CH), F32),
+        vmem((1, MEM), I32),
         vmem((LON, WIDE), BF16),
         vmem((4, 8, WIDE), F32),
         vmem((4, 8, WIDE), F32),
@@ -457,50 +443,50 @@
         vmem((LAT, LAT), BF16),
         vmem((S * COLS, WIDE), BF16),
         vmem((CH, 128), F32),
-        vmem((OWN, 8, 128), F32),
-        vmem((2, 32, 128), F32),
+        vmem((OWN, 8, 256), F32),
+        vmem((S, 8, 256), F32),
+        vmem((S, 8, 256), F32),
+        vmem((TN, PIECE, 128), BF16),
+        vmem((TN - 1, PIECE, 128), BF16),
+        vmem((PIECE, 128), F32),
+        vmem((PIECE, 128), BF16),
+        vmem((TN, PIECE, 128), BF16),
+        vmem((TN * PIECE, ALL * ROWS), BF16),
+        vmem((ALL * ROWS, TN * PIECE), BF16),
     ]
 
     def both(shape, kind):
-        return [vmem(shape(128 * TILES[c], PIECE[c], ROWS * TILES[c]), kind) for c in range(CHUNKS)]
-
-    scratch += both(lambda n, r, h: (4, MEMB, ROWS, n), BF16)
-    scratch += both(lambda n, r, h: (MEMB, ROWS, n), BF16)
-    scratch += both(lambda n, r, h: (4, MEMB, ROWS, n), BF16)
-    scratch += both(lambda n, r, h: (YN, ROWS, n), BF16)
-    scratch += both(lambda n, r, h: (YN - 1, ROWS, n), BF16)
-    scratch += both(lambda n, r, h: (TN, r, 128), BF16)
-    scratch += both(lambda n, r, h: (TN - 1, r, 128), BF16)
-    scratch += both(lambda n, r, h: (r, 128), F32)
-    scratch += both(lambda n, r, h: (r, 128), BF16)
-    scratch += both(lambda n, r, h: (TN, r, 128), BF16)
-    scratch += both(lambda n, r, h: (YN, ROWS, n), BF16)
-    scratch += both(lambda n, r, h: (4, MEMB, ROWS, n), BF16)
-    scratch += both(lambda n, r, h: (MEMB, ROWS, n), BF16)
-    scratch += both(lambda n, r, h: (4, MEMB, ROWS, n), BF16)
-    scratch += both(lambda n, r, h: (2, 4, ROWS, n // 2), BF16)
-    scratch += both(lambda n, r, h: (2, 4, ROWS, n // 2), BF16)
-    scratch += both(lambda n, r, h: (TN * r, h), BF16)
-    scratch += both(lambda n, r, h: (h, TN * r), BF16)
-    scratch += both(lambda n, r, h: (S * ROWS, n), BF16)
+        return [vmem(shape(128 * TILES[c]), kind) for c in range(CHUNKS)]
+
+    scratch += both(lambda n: (4, MEMB, ROWS, n), BF16)
+    scratch += both(lambda n: (MEMB, ROWS, n), BF16)
+    scratch += both(lambda n: (4, MEMB, ROWS, n), BF16)
+    scratch += both(lambda n: (YN, ROWS, n), BF16)
+    scratch += both(lambda n: (YN - 1, ROWS, n), BF16)
+    scratch += both(lambda n: (YN, ROWS, n), BF16)
+    scratch += both(lambda n: (4, MEMB, ROWS, n), BF16)
+    scratch += both(lambda n: (MEMB, ROWS, n), BF16)
+    scratch += both(lambda n: (4, MEMB, ROWS, n), BF16)
+    scratch += both(lambda n: (2, 4, ROWS, n // 2), BF16)
+    scratch += both(lambda n: (2, 4, ROWS, n // 2), BF16)
+    scratch += both(lambda n: (S * ROWS, n), BF16)
     scratch += [
-        dma((8,)), dma((S,)), dma((FIELDS,)),
+        dma((10,)), dma((S,)), dma((FIELDS,)),
         dma((2, 4)), dma((2, 4)), dma((3,)), dma((3,)),
-        dma((2, YN - 1)), dma((2, YN - 1)), dma((2, TN - 1)), dma((2, TN - 1)),
-        dma((2, TN - 1)), dma((2, TN - 1)), dma((2, YN - 1)), dma((2, YN - 1)),
+        dma((2, YN - 1)), dma((2, YN - 1)), dma((TN - 1,)), dma((TN - 1,)),
+        dma((TN - 1,)), dma((TN - 1,)), dma((2, YN - 1)), dma((2, YN - 1)),
         dma((2, 4)), dma((2, 4)), dma((2, YN + 1)), dma((2, YN + 1)),
     ]
-    in_hbm = pl.BlockSpec(memory_space=pl.ANY)
-    in_vmem = pl.BlockSpec(memory_space=pltpu.VMEM)
+    anywhere = pl.BlockSpec(memory_space=pl.ANY)
     return pl.pallas_call(
         kernel,
         out_shape=(jax.ShapeDtypeStruct((MEMB, S, ROWS, LON), F32), jax.ShapeDtypeStruct((S, ROWS, LON), F32)),
-        in_specs=[in_hbm] * len(inputs) + [in_vmem, in_vmem],
-        out_specs=(in_hbm, in_hbm),
+        in_specs=[pl.BlockSpec(memory_space=pltpu.HBM)] * len(inputs),
+        out_specs=(anywhere, anywhere),
         scratch_shapes=scratch,
-        compiler_params=pltpu.CompilerParams(collective_id=0, has_side_effects=True, vmem_limit_bytes=60 << 20),
+        compiler_params=pltpu.CompilerParams(collective_id=0, has_side_effects=True, vmem_limit_bytes=40 << 20),
         name="hessian",
-    )(*inputs, channel_error.reshape(1, CH), member_weight.reshape(1, -1))
+    )(*[pltpu.with_memory_space_constraint(v, pltpu.HBM) for v in inputs])
 
 
 def solution(mesh):

time: 66.9 us -> 68.8 us (1.028)
  Pallas kernels: 62.1 us -> 65.9 us
  local copies, waits for them, and re-layouts: 4.01 us -> 2.22 us
    pallas_call x1, Pallas kernels: 62.1 us -> 65.9 us  [shards(): pl.pallas_call(kernel, out_shape=(jax.ShapeDtypeStruct((MEMB, S, ROWS, LO...]
    unnamed x4 -> x2, local copies, waits for them, and re-layouts: 4.01 us -> 2.22 us
where the time goes in v4:
time: 68.8 us
  Pallas kernels  65.9 us (96%)
  local copies, waits for them, and re-layouts  2.22 us (3%)
    pallas_call x1, Pallas kernels, shards(): pl.pallas_call(kernel, out_shape=(jax.ShapeDtypeStruct((MEMB, S, ROWS, LO...  65.9 us
    unnamed x2, local copies, waits for them, and re-layouts  2.22 us

profile of v4, /device:TPU:1, one launch (start us, length us, event | category | flops | bytes accessed | tf_op | source)
XLA Modules:
  0.0 68.8 jit_solution(10526709858787481157)
XLA Ops:
  0.6 65.9 %hessian.1 = (f32[2,4,80,720]{3,2,1,0:T(8,128)S(1)}, f32[4,80,720]{2,1,0:T(8,128)S(1)}) custom-call(bf16[2,4,80,720]{3,2,1,0:T(8,128)(2,1)} %alpha_hbm.1, bf16[4,80,720]{2,1,0:T(8,128)(2,1)} %static_hbm.1, bf16[2,180,4,320]{3,2,1,0:T(4,128)(2,1)} %bitcast.6, f32[180,4,320]{2,1,0:T(4,128)} %bitcast.7, bf16[720,720]{1,0:T(8,128)(2,1)} %lon_hbm.1, ...), custom_call_target="tpu_custom_call" | custom-call | tf_op jit(solution)/shard_map/hessian/pallas_call | solution.py:481
  66.5 1.3 %copy.15 = f32[2,4,80,720]{3,2,1,0:T(8,128)} copy(f32[2,4,80,720]{3,2,1,0:T(8,128)S(1)} %get-tuple-element.4) | data formatting | bytes 3686400
  67.8 0.9 %copy.16 = f32[4,80,720]{2,1,0:T(8,128)} copy(f32[4,80,720]{2,1,0:T(8,128)S(1)} %get-tuple-element.5) | data formatting | bytes 1843200

commit v5 on v3

--- a/solution.py
+++ b/solution.py
@@ -10,7 +10,7 @@
 MESH = pl.DeviceIdType.MESH
 F32, BF16, I32 = jnp.float32, jnp.bfloat16, jnp.int32
 
-S, CH, MEMB, FIELDS = 4, 32, 2, 3
+S, CH, MEM, MEMB, FIELDS = 4, 32, 128, 2, 3
 ROWS, LAT, LON, COLS = 80, 320, 720, 180
 REM = COLS - 128
 YN, TN, OWN = 4, 16, 5
@@ -68,9 +68,9 @@
 
 
 def kernel(
-    alpha_hbm, static_hbm, pert_hbm, std_hbm, lon_hbm, lat_hbm, jac_hbm, count_hbm, mask_hbm, error_ref, weight_ref,
+    alpha_hbm, static_hbm, pert_hbm, std_hbm, lon_hbm, lat_hbm, jac_hbm, count_hbm, mask_hbm, error_hbm, weight_hbm,
     ga_hbm, gs_hbm,
-    alpha, static, pert, std, lon, lat, jac, count, mask,
+    alpha, static, pert, std, lon, lat, jac, count, mask, error_row, weight_row,
     w, ss, sr, out, spread, rem, order, latp, latpt, spreader, squares, incs, gr,
     fs0, fs1, rl0, rl1, xr0, xr1, rs0, rs1, r10, r11, s20, s21, r20, r21, terms0, terms1, gp0, gp1, gz0, gz1, ag0, ag1,
     bs0, bs1, bl0, bl1, br0, br1, bss0, bss1, brs0, brs1, to0, to1, from0, from1, lhs0, lhs1,
@@ -97,7 +97,8 @@
     to_t = [{"mem": 8 * (v // 2) + 4 * (v % 2) + y, "band": band} for v in ts]
 
     staged = [(lon_hbm, lon), (alpha_hbm, alpha), (static_hbm, static), (lat_hbm, lat),
-              (pert_hbm.reshape(MEMB, S * COLS, LAT), pert), (jac_hbm, jac), (count_hbm, count), (mask_hbm, mask)]
+              (pert_hbm.reshape(MEMB, S * COLS, LAT), pert), (jac_hbm, jac), (count_hbm, count), (mask_hbm, mask),
+              (error_hbm, error_row), (weight_hbm, weight_row)]
     loads = [pltpu.make_async_copy(src, dst, load_sem.at[i]) for i, (src, dst) in enumerate(staged)]
     loads += [pltpu.make_async_copy(std_hbm.at[:, s, :], std.at[s], std_sem.at[s]) for s in range(S)]
     for load in loads:
@@ -142,21 +143,12 @@
             remote(fs[c].at[sib], xr[c].at[band], f_send.at[c, 2], f_recv.at[c, 2], at_band(sib)),
             remote(rl[c], xr[c].at[sib], f_send.at[c, 3], f_recv.at[c, 3], at_band(far)),
         ]
-        if c == 0:
-            pl.semaphore_wait(barrier, len(partners))
-        else:
-            forward[0][1].wait_recv()
-            forward[0][3].start()
-        for copy in copies[:3]:
-            copy.start()
         forward.append(copies)
         xr[c][band] = fs[c][band]
 
     loads[2].wait()
     loads[3].wait()
     v = dot(static[...].reshape(S * ROWS, LON), w[...]).astype(BF16)
-    forward[1][1].wait_recv()
-    forward[1][3].start()
     own_rows = dot(one_hot(16, LAT, lambda k: jnp.where(k < OWN, OWN * mem + k, -1)), lat[...]).astype(BF16)
     here = jnp.where(iota((LAT, ROWS), 0) == ROWS * band + iota((LAT, ROWS), 1), 1.0, 0.0).astype(BF16)
     own_part = dot(own_rows, here).astype(BF16)
@@ -171,14 +163,22 @@
                 parts[2 * h][:, tile : tile + 128], parts[2 * h + 1][:, tile : tile + 128])
     others = (far, cross, sib)
     static_copies = [remote(ss.at[b], sr.at[band], t_send.at[k], t_recv.at[k], at_band(b)) for k, b in enumerate(others)]
-    for copy in static_copies:
-        copy.start()
     sr[band] = ss[band]
-
     order[...] = one_hot(LAT, LAT, grid_row)
     latp[...] = dot(order[...], lat[...]).astype(BF16)
+    pl.semaphore_wait(barrier, len(partners))
+    for copy in forward[0][:3] + [forward[1][1]] + static_copies:
+        copy.start()
+    forward[0][1].wait_recv()
+    forward[0][3].start()
+    forward[1][0].start()
+    forward[1][1].wait_recv()
+    forward[1][3].start()
+    forward[1][2].start()
+
     spreader[...] = one_hot(S * COLS, WIDE, packed_lane)
-    weights = weight_ref[...].astype(F32)
+    loads[9].wait()
+    weights = weight_row[...].astype(F32)
     coef = weights / jnp.sqrt(jnp.sum(weights * weights, axis=1, keepdims=True))
     loads[4].wait()
     for m in range(MEMB):
@@ -312,16 +312,9 @@
             brs[c][h, band] = bss[c][h, band]
         return copies, fixed
 
-    def pass_on(c, copies, fixed):
-        copies[1].wait_recv()
-        copies[3].start()
-        fixed[0].wait_recv()
-        for copy in fixed[2:]:
-            copy.start()
-
     first = [sum_first(0)]
 
-    for load in loads[8:]:
+    for load in loads[10:]:
         load.wait()
     rem[...] = jnp.zeros_like(rem)
     for h in range(2):
@@ -338,7 +331,6 @@
             rem[s, :, 0:REM] = ordered[:, 128:COLS]
         spread[MEMB, 0:LAT, 512 + 128 * h : 640 + 128 * h] = joined(rem[0], rem[1])
 
-    first.append(sum_first(1))
     spread[:, LAT:] = jnp.zeros((FIELDS, 8, WIDE), F32)
     first_row = ROWS * y + OWN * t
     shift = first_row % 8
@@ -352,6 +344,10 @@
         terms[c][...] = jnp.zeros_like(terms[c])
         for l in range(TILES[c]):
             terms[c][OWN * l : OWN * l + OWN] = static_term[0:OWN, BASE[c] + 128 * l : BASE[c] + 128 * l + 128]
+    for load in loads[5:9]:
+        load.wait()
+    error = jnp.sum(jnp.where(iota((CH, CH), 0) == iota((CH, CH), 1), error_row[...], 0.0), axis=1, keepdims=True)
+    squares[...] = jnp.broadcast_to(error * error, squares.shape)
 
     second = [sum_second(0, first[0])]
     latpt[...] = dot(jnp.transpose(lat[...].astype(F32)).astype(BF16), order[...], (1, 1)).astype(BF16)
@@ -359,23 +355,25 @@
         rows, height = TN * PIECE[c], ROWS * TILES[c]
         hot = iota((height, rows), 0) == piece_row(c, iota((height, rows), 1))
         from_piece[c][...] = jnp.where(hot, 1.0, 0.0).astype(BF16)
-    error = jnp.sum(jnp.where(iota((CH, CH), 0) == iota((CH, CH), 1), error_ref[...], 0.0), axis=1, keepdims=True)
-    squares[...] = jnp.broadcast_to(error * error, squares.shape)
-    for load in loads[5:8]:
-        load.wait()
+
+    first.append(sum_first(1))
+
+    third = [pixels(0, second[0])]
 
     second.append(sum_second(1, first[1]))
 
-    third = [pixels(0, second[0])]
+    fourth = [gather(0, third[0])]
 
     third.append(pixels(1, second[1]))
 
-    fourth = [gather(0, third[0])]
+    ways = [adjoint(0, fourth[0])]
+    ways[0][0][1].wait_recv()
+    ways[0][0][3].start()
 
     fourth.append(gather(1, third[1]))
-
-    ways = [adjoint(0, fourth[0])]
-    pass_on(0, *ways[0])
+    ways[0][1][0].wait_recv()
+    for copy in ways[0][1][2:]:
+        copy.start()
 
     ways.append(adjoint(1, fourth[1]))
 
@@ -434,7 +432,8 @@
 def shards(alpha, static_ctl, perturbations, static_std, lon_root, lat_root, jacobian, obs_count, channel_mask,
            channel_error, member_weight):
     inputs = [alpha, static_ctl, jnp.transpose(perturbations, (0, 3, 1, 2)), jnp.transpose(static_std, (2, 0, 1)),
-              lon_root, lat_root, jnp.transpose(jacobian, (0, 2, 1, 3)), obs_count, jnp.transpose(channel_mask, (1, 0, 2))]
+              lon_root, lat_root, jnp.transpose(jacobian, (0, 2, 1, 3)), obs_count, jnp.transpose(channel_mask, (1, 0, 2)),
+              channel_error.reshape(1, CH), member_weight.reshape(1, MEM)]
     dma, vmem = pltpu.SemaphoreType.DMA, pltpu.VMEM
     scratch = [
         vmem((MEMB, S, ROWS, LON), BF16),
@@ -446,6 +445,8 @@
         vmem((CH, OWN, S, COLS), BF16),
         vmem((OWN, COLS), I32),
         vmem((OWN, CH, COLS), I32),
+        vmem((1, CH), F32),
+        vmem((1, MEM), I32),
         vmem((LON, WIDE), BF16),
         vmem((4, 8, WIDE), F32),
         vmem((4, 8, WIDE), F32),
@@ -484,23 +485,22 @@
     scratch += both(lambda n, r, h: (h, TN * r), BF16)
     scratch += both(lambda n, r, h: (S * ROWS, n), BF16)
     scratch += [
-        dma((8,)), dma((S,)), dma((FIELDS,)),
+        dma((10,)), dma((S,)), dma((FIELDS,)),
         dma((2, 4)), dma((2, 4)), dma((3,)), dma((3,)),
         dma((2, YN - 1)), dma((2, YN - 1)), dma((2, TN - 1)), dma((2, TN - 1)),
         dma((2, TN - 1)), dma((2, TN - 1)), dma((2, YN - 1)), dma((2, YN - 1)),
         dma((2, 4)), dma((2, 4)), dma((2, YN + 1)), dma((2, YN + 1)),
     ]
-    in_hbm = pl.BlockSpec(memory_space=pl.ANY)
-    in_vmem = pl.BlockSpec(memory_space=pltpu.VMEM)
+    anywhere = pl.BlockSpec(memory_space=pl.ANY)
     return pl.pallas_call(
         kernel,
         out_shape=(jax.ShapeDtypeStruct((MEMB, S, ROWS, LON), F32), jax.ShapeDtypeStruct((S, ROWS, LON), F32)),
-        in_specs=[in_hbm] * len(inputs) + [in_vmem, in_vmem],
-        out_specs=(in_hbm, in_hbm),
+        in_specs=[pl.BlockSpec(memory_space=pltpu.HBM)] * len(inputs),
+        out_specs=(anywhere, anywhere),
         scratch_shapes=scratch,
-        compiler_params=pltpu.CompilerParams(collective_id=0, has_side_effects=True, vmem_limit_bytes=60 << 20),
+        compiler_params=pltpu.CompilerParams(collective_id=0, has_side_effects=True, vmem_limit_bytes=40 << 20),
         name="hessian",
-    )(*inputs, channel_error.reshape(1, CH), member_weight.reshape(1, -1))
+    )(*[pltpu.with_memory_space_constraint(v, pltpu.HBM) for v in inputs])
 
 
 def solution(mesh):

time: 66.9 us -> 65.6 us (0.981)
  local copies, waits for them, and re-layouts: 4.01 us -> 2.22 us
    unnamed x4 -> x2, local copies, waits for them, and re-layouts: 4.01 us -> 2.22 us
where the time goes in v5:
time: 65.6 us; the launch traced here: 65.5 us
  Pallas kernels  62.6 us (95%)
  local copies, waits for them, and re-layouts  2.22 us (3%)
    pallas_call x1, Pallas kernels, shards(): pl.pallas_call(kernel, out_shape=(jax.ShapeDtypeStruct((MEMB, S, ROWS, LO...  62.6 us
    unnamed x2, local copies, waits for them, and re-layouts  2.22 us

profile of v5, /device:TPU:1, one launch (start us, length us, event | category | flops | bytes accessed | tf_op | source)
XLA Modules:
  0.0 65.5 jit_solution(8682685191521085997)
XLA Ops:
  0.6 62.6 %hessian.1 = (f32[2,4,80,720]{3,2,1,0:T(8,128)S(1)}, f32[4,80,720]{2,1,0:T(8,128)S(1)}) custom-call(bf16[2,4,80,720]{3,2,1,0:T(8,128)(2,1)} %alpha_hbm.1, bf16[4,80,720]{2,1,0:T(8,128)(2,1)} %static_hbm.1, bf16[2,180,4,320]{3,2,1,0:T(4,128)(2,1)} %bitcast.6, f32[180,4,320]{2,1,0:T(4,128)} %bitcast.7, bf16[720,720]{1,0:T(8,128)(2,1)} %lon_hbm.1, ...), custom_call_target="tpu_custom_call" | custom-call | tf_op jit(solution)/shard_map/hessian/pallas_call | solution.py:495
  63.3 1.3 %copy.15 = f32[2,4,80,720]{3,2,1,0:T(8,128)} copy(f32[2,4,80,720]{3,2,1,0:T(8,128)S(1)} %get-tuple-element.4) | data formatting | bytes 3686400
  64.5 0.9 %copy.16 = f32[4,80,720]{2,1,0:T(8,128)} copy(f32[4,80,720]{2,1,0:T(8,128)S(1)} %get-tuple-element.5) | data formatting | bytes 1843200

commit v6 on v5

--- a/solution.py
+++ b/solution.py
@@ -15,6 +15,7 @@
 REM = COLS - 128
 YN, TN, OWN = 4, 16, 5
 WIDE = 768
+NEXT_Y, NEXT_T = (2, 1, 3), (8, 7, 9, 6, 10, 5, 11, 4, 12, 3, 13, 2, 14, 1, 15)
 CHUNKS = 2
 TILES = (2, 4)
 BASE = (512, 0)
@@ -91,9 +92,9 @@
     def at_band(b):
         return {"mem": mem, "band": b}
 
-    ys = [lax.rem(y + k, YN) for k in range(1, YN)]
+    ys = [lax.rem(y + k, YN) for k in NEXT_Y]
     to_y = [{"mem": 8 * z + 4 * x + v, "band": band} for v in ys]
-    ts = [lax.rem(t + k, TN) for k in range(1, TN)]
+    ts = [lax.rem(t + k, TN) for k in NEXT_T]
     to_t = [{"mem": 8 * (v // 2) + 4 * (v % 2) + y, "band": band} for v in ts]
 
     staged = [(lon_hbm, lon), (alpha_hbm, alpha), (static_hbm, static), (lat_hbm, lat),
@@ -105,7 +106,7 @@
         load.start()
 
     barrier = pltpu.get_barrier_semaphore()
-    partners = [at_band(far), at_band(cross)] + to_t + to_y + [at_band(sib)]
+    partners = to_t + to_y + [at_band(far), at_band(cross), at_band(sib)]
     for device in partners:
         pl.semaphore_signal(barrier, inc=1, device_id=device, device_id_type=MESH)
 
@@ -350,14 +351,14 @@
     squares[...] = jnp.broadcast_to(error * error, squares.shape)
 
     second = [sum_second(0, first[0])]
+
+    first.append(sum_first(1))
     latpt[...] = dot(jnp.transpose(lat[...].astype(F32)).astype(BF16), order[...], (1, 1)).astype(BF16)
     for c in range(CHUNKS):
         rows, height = TN * PIECE[c], ROWS * TILES[c]
         hot = iota((height, rows), 0) == piece_row(c, iota((height, rows), 1))
         from_piece[c][...] = jnp.where(hot, 1.0, 0.0).astype(BF16)
 
-    first.append(sum_first(1))
-
     third = [pixels(0, second[0])]
 
     second.append(sum_second(1, first[1]))
@@ -376,11 +377,16 @@
         copy.start()
 
     ways.append(adjoint(1, fourth[1]))
+    ways[1][0][1].wait_recv()
+    ways[1][0][3].start()
 
     copies, fixed = ways[0]
-    for copy in copies[:1] + copies[2:] + fixed[1:]:
+    for copy in copies[:1] + copies[2:]:
         copy.wait_recv()
     for f in range(FIELDS):
+        if f == MEMB:
+            for copy in fixed[1:]:
+                copy.wait_recv()
         for h in range(2):
             if f < MEMB:
                 tiles = [br[0][b, f, :, 128 * h : 128 * h + 128].astype(F32) for b in range(4)]
@@ -393,12 +399,10 @@
                     lhs[0][pl.ds((2 * h + s) * ROWS, ROWS), 128 * g : 128 * g + 128] = pair
         base = alpha[f] if f < MEMB else static[...]
         out[f] = base.astype(F32) + dot(lhs[0][...], w[:, lanes[0]], (1, 1)).reshape(S, ROWS, LON)
-        if f == 0:
-            ways[1][0][1].wait_recv()
-            ways[1][0][3].start()
-    ways[1][1][0].wait_recv()
-    for copy in ways[1][1][2:]:
-        copy.start()
+        if f == MEMB - 1:
+            ways[1][1][0].wait_recv()
+            for copy in ways[1][1][2:]:
+                copy.start()
 
     stores = []
     copies, fixed = ways[1]

time: 65.6 us -> 63.7 us (0.971)
  Pallas kernels: 62.6 us -> 60.8 us
    pallas_call x1, Pallas kernels: 62.6 us -> 60.8 us  [shards(): pl.pallas_call(kernel, out_shape=(jax.ShapeDtypeStruct((MEMB, S, ROWS, LO...]
where the time goes in v6:
time: 63.7 us; the launch traced here: 63.6 us
  Pallas kernels  60.8 us (95%)
  local copies, waits for them, and re-layouts  2.22 us (3%)
  between operations  0.64 us (1%)
    pallas_call x1, Pallas kernels, shards(): pl.pallas_call(kernel, out_shape=(jax.ShapeDtypeStruct((MEMB, S, ROWS, LO...  60.8 us
    unnamed x2, local copies, waits for them, and re-layouts  2.22 us

profile of v6, /device:TPU:1, one launch (start us, length us, event | category | flops | bytes accessed | tf_op | source)
XLA Modules:
  0.0 63.6 jit_solution(11074265556936441509)
XLA Ops:
  0.6 60.8 %hessian.1 = (f32[2,4,80,720]{3,2,1,0:T(8,128)S(1)}, f32[4,80,720]{2,1,0:T(8,128)S(1)}) custom-call(bf16[2,4,80,720]{3,2,1,0:T(8,128)(2,1)} %alpha_hbm.1, bf16[4,80,720]{2,1,0:T(8,128)(2,1)} %static_hbm.1, bf16[2,180,4,320]{3,2,1,0:T(4,128)(2,1)} %bitcast.6, f32[180,4,320]{2,1,0:T(4,128)} %bitcast.7, bf16[720,720]{1,0:T(8,128)(2,1)} %lon_hbm.1, ...), custom_call_target="tpu_custom_call" | custom-call | tf_op jit(solution)/shard_map/hessian/pallas_call | solution.py:499
  61.4 1.3 %copy.15 = f32[2,4,80,720]{3,2,1,0:T(8,128)} copy(f32[2,4,80,720]{3,2,1,0:T(8,128)S(1)} %get-tuple-element.4) | data formatting | bytes 3686400
  62.7 0.9 %copy.16 = f32[4,80,720]{2,1,0:T(8,128)} copy(f32[4,80,720]{2,1,0:T(8,128)S(1)} %get-tuple-element.5) | data formatting | bytes 1843200

commit v7 on v6

--- a/solution.py
+++ b/solution.py
@@ -70,12 +70,12 @@
 
 def kernel(
     alpha_hbm, static_hbm, pert_hbm, std_hbm, lon_hbm, lat_hbm, jac_hbm, count_hbm, mask_hbm, error_hbm, weight_hbm,
-    ga_hbm, gs_hbm,
+    ga, gs,
     alpha, static, pert, std, lon, lat, jac, count, mask, error_row, weight_row,
-    w, ss, sr, out, spread, rem, order, latp, latpt, spreader, squares, incs, gr,
+    w, ss, sr, spread, rem, order, latp, latpt, spreader, squares, incs, gr,
     fs0, fs1, rl0, rl1, xr0, xr1, rs0, rs1, r10, r11, s20, s21, r20, r21, terms0, terms1, gp0, gp1, gz0, gz1, ag0, ag1,
     bs0, bs1, bl0, bl1, br0, br1, bss0, bss1, brs0, brs1, to0, to1, from0, from1, lhs0, lhs1,
-    load_sem, std_sem, store_sem, f_send, f_recv, t_send, t_recv, a_send, a_recv, b_send, b_recv, c_send, c_recv,
+    load_sem, std_sem, f_send, f_recv, t_send, t_recv, a_send, a_recv, b_send, b_recv, c_send, c_recv,
     d_send, d_recv, e_send, e_recv, g_send, g_recv,
 ):
     fs, rl, xr, rs, r1, s2, r2 = (fs0, fs1), (rl0, rl1), (xr0, xr1), (rs0, rs1), (r10, r11), (s20, s21), (r20, r21)
@@ -168,14 +168,14 @@
     order[...] = one_hot(LAT, LAT, grid_row)
     latp[...] = dot(order[...], lat[...]).astype(BF16)
     pl.semaphore_wait(barrier, len(partners))
-    for copy in forward[0][:3] + [forward[1][1]] + static_copies:
+    for copy in forward[1][:3] + [forward[0][1]] + static_copies:
         copy.start()
+    forward[1][1].wait_recv()
+    forward[1][3].start()
+    forward[0][0].start()
     forward[0][1].wait_recv()
     forward[0][3].start()
-    forward[1][0].start()
-    forward[1][1].wait_recv()
-    forward[1][3].start()
-    forward[1][2].start()
+    forward[0][2].start()
 
     spreader[...] = one_hot(S * COLS, WIDE, packed_lane)
     loads[9].wait()
@@ -313,7 +313,7 @@
             brs[c][h, band] = bss[c][h, band]
         return copies, fixed
 
-    first = [sum_first(0)]
+    first = {1: sum_first(1)}
 
     for load in loads[10:]:
         load.wait()
@@ -350,42 +350,63 @@
     error = jnp.sum(jnp.where(iota((CH, CH), 0) == iota((CH, CH), 1), error_row[...], 0.0), axis=1, keepdims=True)
     squares[...] = jnp.broadcast_to(error * error, squares.shape)
 
-    second = [sum_second(0, first[0])]
-
-    first.append(sum_first(1))
+    second = {1: sum_second(1, first[1])}
+
+    first[0] = sum_first(0)
     latpt[...] = dot(jnp.transpose(lat[...].astype(F32)).astype(BF16), order[...], (1, 1)).astype(BF16)
     for c in range(CHUNKS):
         rows, height = TN * PIECE[c], ROWS * TILES[c]
         hot = iota((height, rows), 0) == piece_row(c, iota((height, rows), 1))
         from_piece[c][...] = jnp.where(hot, 1.0, 0.0).astype(BF16)
 
-    third = [pixels(0, second[0])]
-
-    second.append(sum_second(1, first[1]))
-
-    fourth = [gather(0, third[0])]
-
-    third.append(pixels(1, second[1]))
-
-    ways = [adjoint(0, fourth[0])]
-    ways[0][0][1].wait_recv()
-    ways[0][0][3].start()
-
-    fourth.append(gather(1, third[1]))
-    ways[0][1][0].wait_recv()
-    for copy in ways[0][1][2:]:
+    second[0] = sum_second(0, first[0])
+
+    third = {1: pixels(1, second[1])}
+
+    third[0] = pixels(0, second[0])
+
+    fourth = {1: gather(1, third[1])}
+
+    fourth[0] = gather(0, third[0])
+
+    copies, fixed = adjoint(1, fourth[1])
+    copies[1].wait_recv()
+    copies[3].start()
+
+    last, last_fixed = adjoint(0, fourth[0])
+    fixed[0].wait_recv()
+    for copy in fixed[2:]:
         copy.start()
-
-    ways.append(adjoint(1, fourth[1]))
-    ways[1][0][1].wait_recv()
-    ways[1][0][3].start()
-
-    copies, fixed = ways[0]
+    last[1].wait_recv()
+    last[3].start()
+
+    def result(f):
+        return ga.at[f] if f < MEMB else gs
+
     for copy in copies[:1] + copies[2:]:
         copy.wait_recv()
     for f in range(FIELDS):
         if f == MEMB:
+            last_fixed[0].wait_recv()
+            for copy in last_fixed[2:]:
+                copy.start()
             for copy in fixed[1:]:
+                copy.wait_recv()
+        for s in range(S):
+            for b in range(4):
+                if f < MEMB:
+                    tile = br[1][b, f, :, 128 * s : 128 * s + 128]
+                else:
+                    tile = brs[1][s // 2, b, :, 128 * (s % 2) : 128 * (s % 2) + 128]
+                lhs[1][ROWS * s : ROWS * s + ROWS, 128 * b : 128 * b + 128] = tile
+        base = alpha[f] if f < MEMB else static[...]
+        result(f)[...] = base.astype(F32) + dot(lhs[1][...], w[:, lanes[1]], (1, 1)).reshape(S, ROWS, LON)
+
+    for copy in last[:1] + last[2:]:
+        copy.wait_recv()
+    for f in range(FIELDS):
+        if f == MEMB:
+            for copy in last_fixed[1:]:
                 copy.wait_recv()
         for h in range(2):
             if f < MEMB:
@@ -397,39 +418,8 @@
                 for g in range(2):
                     pair = join(tiles[2 * g], tiles[2 * g + 1]).astype(BF16)
                     lhs[0][pl.ds((2 * h + s) * ROWS, ROWS), 128 * g : 128 * g + 128] = pair
-        base = alpha[f] if f < MEMB else static[...]
-        out[f] = base.astype(F32) + dot(lhs[0][...], w[:, lanes[0]], (1, 1)).reshape(S, ROWS, LON)
-        if f == MEMB - 1:
-            ways[1][1][0].wait_recv()
-            for copy in ways[1][1][2:]:
-                copy.start()
-
-    stores = []
-    copies, fixed = ways[1]
-    for f in range(FIELDS):
-        if f == 0:
-            for copy in copies[:1] + copies[2:]:
-                copy.wait_recv()
-        if f == MEMB:
-            for copy in fixed[1:]:
-                copy.wait_recv()
-        for s in range(S):
-            for b in range(4):
-                if f < MEMB:
-                    tile = br[1][b, f, :, 128 * s : 128 * s + 128]
-                else:
-                    tile = brs[1][s // 2, b, :, 128 * (s % 2) : 128 * (s % 2) + 128]
-                lhs[1][ROWS * s : ROWS * s + ROWS, 128 * b : 128 * b + 128] = tile
-        out[f] = out[f] + dot(lhs[1][...], w[:, lanes[1]], (1, 1)).reshape(S, ROWS, LON)
-        store = pltpu.make_async_copy(out.at[f], ga_hbm.at[f] if f < MEMB else gs_hbm, store_sem.at[f])
-        store.start()
-        stores.append(store)
-    for copies, fixed in ways:
-        sent.extend(copies)
-        sent.extend(fixed)
-    for store in stores:
-        store.wait()
-    for copy in sent:
+        result(f)[...] = result(f)[...] + dot(lhs[0][...], w[:, lanes[0]], (1, 1)).reshape(S, ROWS, LON)
+    for copy in sent + copies + fixed + last + last_fixed:
         copy.wait_send()
 
 
@@ -454,7 +444,6 @@
         vmem((LON, WIDE), BF16),
         vmem((4, 8, WIDE), F32),
         vmem((4, 8, WIDE), F32),
-        vmem((FIELDS, S, ROWS, LON), F32),
         vmem((FIELDS, LAT + 8, WIDE), F32),
         vmem((2, LAT, 128), F32),
         vmem((LAT, LAT), BF16),
@@ -489,18 +478,17 @@
     scratch += both(lambda n, r, h: (h, TN * r), BF16)
     scratch += both(lambda n, r, h: (S * ROWS, n), BF16)
     scratch += [
-        dma((10,)), dma((S,)), dma((FIELDS,)),
+        dma((10,)), dma((S,)),
         dma((2, 4)), dma((2, 4)), dma((3,)), dma((3,)),
         dma((2, YN - 1)), dma((2, YN - 1)), dma((2, TN - 1)), dma((2, TN - 1)),
         dma((2, TN - 1)), dma((2, TN - 1)), dma((2, YN - 1)), dma((2, YN - 1)),
         dma((2, 4)), dma((2, 4)), dma((2, YN + 1)), dma((2, YN + 1)),
     ]
-    anywhere = pl.BlockSpec(memory_space=pl.ANY)
     return pl.pallas_call(
         kernel,
         out_shape=(jax.ShapeDtypeStruct((MEMB, S, ROWS, LON), F32), jax.ShapeDtypeStruct((S, ROWS, LON), F32)),
         in_specs=[pl.BlockSpec(memory_space=pltpu.HBM)] * len(inputs),
-        out_specs=(anywhere, anywhere),
+        out_specs=(pl.BlockSpec(memory_space=pltpu.VMEM),) * 2,
         scratch_shapes=scratch,
         compiler_params=pltpu.CompilerParams(collective_id=0, has_side_effects=True, vmem_limit_bytes=40 << 20),
         name="hessian",

time: 63.7 us -> 64.6 us (1.014)
  Pallas kernels: 60.8 us -> 61.6 us
    pallas_call x1, Pallas kernels: 60.8 us -> 61.6 us  [shards(): pl.pallas_call(kernel, out_shape=(jax.ShapeDtypeStruct((MEMB, S, ROWS, LO...]
where the time goes in v7:
time: 64.6 us; the launch traced here: 64.5 us
  Pallas kernels  61.6 us (95%)
  local copies, waits for them, and re-layouts  2.22 us (3%)
    pallas_call x1, Pallas kernels, shards(): pl.pallas_call(kernel, out_shape=(jax.ShapeDtypeStruct((MEMB, S, ROWS, LO...  61.6 us
    unnamed x2, local copies, waits for them, and re-layouts  2.22 us

profile of v7, /device:TPU:1, one launch (start us, length us, event | category | flops | bytes accessed | tf_op | source)
XLA Modules:
  0.0 64.5 jit_solution(5677762356076209487)
XLA Ops:
  0.6 61.6 %hessian.1 = (f32[2,4,80,720]{3,2,1,0:T(8,128)S(1)}, f32[4,80,720]{2,1,0:T(8,128)S(1)}) custom-call(bf16[2,4,80,720]{3,2,1,0:T(8,128)(2,1)} %alpha_hbm.1, bf16[4,80,720]{2,1,0:T(8,128)(2,1)} %static_hbm.1, bf16[2,180,4,320]{3,2,1,0:T(4,128)(2,1)} %bitcast.6, f32[180,4,320]{2,1,0:T(4,128)} %bitcast.7, bf16[720,720]{1,0:T(8,128)(2,1)} %lon_hbm.1, ...), custom_call_target="tpu_custom_call" | custom-call | tf_op jit(solution)/shard_map/hessian/pallas_call | solution.py:487
  62.3 1.3 %copy.15 = f32[2,4,80,720]{3,2,1,0:T(8,128)} copy(f32[2,4,80,720]{3,2,1,0:T(8,128)S(1)} %get-tuple-element.4) | data formatting | bytes 3686400
  63.6 0.9 %copy.16 = f32[4,80,720]{2,1,0:T(8,128)} copy(f32[4,80,720]{2,1,0:T(8,128)S(1)} %get-tuple-element.5) | data formatting | bytes 1843200

commit v8 on v6

--- a/solution.py
+++ b/solution.py
@@ -70,12 +70,12 @@
 
 def kernel(
     alpha_hbm, static_hbm, pert_hbm, std_hbm, lon_hbm, lat_hbm, jac_hbm, count_hbm, mask_hbm, error_hbm, weight_hbm,
-    ga_hbm, gs_hbm,
+    ga, gs,
     alpha, static, pert, std, lon, lat, jac, count, mask, error_row, weight_row,
-    w, ss, sr, out, spread, rem, order, latp, latpt, spreader, squares, incs, gr,
+    w, ss, sr, spread, rem, order, latp, latpt, spreader, squares, incs, gr,
     fs0, fs1, rl0, rl1, xr0, xr1, rs0, rs1, r10, r11, s20, s21, r20, r21, terms0, terms1, gp0, gp1, gz0, gz1, ag0, ag1,
     bs0, bs1, bl0, bl1, br0, br1, bss0, bss1, brs0, brs1, to0, to1, from0, from1, lhs0, lhs1,
-    load_sem, std_sem, store_sem, f_send, f_recv, t_send, t_recv, a_send, a_recv, b_send, b_recv, c_send, c_recv,
+    load_sem, std_sem, f_send, f_recv, t_send, t_recv, a_send, a_recv, b_send, b_recv, c_send, c_recv,
     d_send, d_recv, e_send, e_recv, g_send, g_recv,
 ):
     fs, rl, xr, rs, r1, s2, r2 = (fs0, fs1), (rl0, rl1), (xr0, xr1), (rs0, rs1), (r10, r11), (s20, s21), (r20, r21)
@@ -380,6 +380,7 @@
     ways[1][0][1].wait_recv()
     ways[1][0][3].start()
 
+    result = [ga.at[0], ga.at[1], gs]
     copies, fixed = ways[0]
     for copy in copies[:1] + copies[2:]:
         copy.wait_recv()
@@ -398,13 +399,12 @@
                     pair = join(tiles[2 * g], tiles[2 * g + 1]).astype(BF16)
                     lhs[0][pl.ds((2 * h + s) * ROWS, ROWS), 128 * g : 128 * g + 128] = pair
         base = alpha[f] if f < MEMB else static[...]
-        out[f] = base.astype(F32) + dot(lhs[0][...], w[:, lanes[0]], (1, 1)).reshape(S, ROWS, LON)
+        result[f][...] = base.astype(F32) + dot(lhs[0][...], w[:, lanes[0]], (1, 1)).reshape(S, ROWS, LON)
         if f == MEMB - 1:
             ways[1][1][0].wait_recv()
             for copy in ways[1][1][2:]:
                 copy.start()
 
-    stores = []
     copies, fixed = ways[1]
     for f in range(FIELDS):
         if f == 0:
@@ -420,15 +420,10 @@
                 else:
                     tile = brs[1][s // 2, b, :, 128 * (s % 2) : 128 * (s % 2) + 128]
                 lhs[1][ROWS * s : ROWS * s + ROWS, 128 * b : 128 * b + 128] = tile
-        out[f] = out[f] + dot(lhs[1][...], w[:, lanes[1]], (1, 1)).reshape(S, ROWS, LON)
-        store = pltpu.make_async_copy(out.at[f], ga_hbm.at[f] if f < MEMB else gs_hbm, store_sem.at[f])
-        store.start()
-        stores.append(store)
+        result[f][...] = result[f][...] + dot(lhs[1][...], w[:, lanes[1]], (1, 1)).reshape(S, ROWS, LON)
     for copies, fixed in ways:
         sent.extend(copies)
         sent.extend(fixed)
-    for store in stores:
-        store.wait()
     for copy in sent:
         copy.wait_send()
 
@@ -454,7 +449,6 @@
         vmem((LON, WIDE), BF16),
         vmem((4, 8, WIDE), F32),
         vmem((4, 8, WIDE), F32),
-        vmem((FIELDS, S, ROWS, LON), F32),
         vmem((FIELDS, LAT + 8, WIDE), F32),
         vmem((2, LAT, 128), F32),
         vmem((LAT, LAT), BF16),
@@ -489,18 +483,17 @@
     scratch += both(lambda n, r, h: (h, TN * r), BF16)
     scratch += both(lambda n, r, h: (S * ROWS, n), BF16)
     scratch += [
-        dma((10,)), dma((S,)), dma((FIELDS,)),
+        dma((10,)), dma((S,)),
         dma((2, 4)), dma((2, 4)), dma((3,)), dma((3,)),
         dma((2, YN - 1)), dma((2, YN - 1)), dma((2, TN - 1)), dma((2, TN - 1)),
         dma((2, TN - 1)), dma((2, TN - 1)), dma((2, YN - 1)), dma((2, YN - 1)),
         dma((2, 4)), dma((2, 4)), dma((2, YN + 1)), dma((2, YN + 1)),
     ]
-    anywhere = pl.BlockSpec(memory_space=pl.ANY)
     return pl.pallas_call(
         kernel,
         out_shape=(jax.ShapeDtypeStruct((MEMB, S, ROWS, LON), F32), jax.ShapeDtypeStruct((S, ROWS, LON), F32)),
         in_specs=[pl.BlockSpec(memory_space=pltpu.HBM)] * len(inputs),
-        out_specs=(anywhere, anywhere),
+        out_specs=(pl.BlockSpec(memory_space=pltpu.VMEM),) * 2,
         scratch_shapes=scratch,
         compiler_params=pltpu.CompilerParams(collective_id=0, has_side_effects=True, vmem_limit_bytes=40 << 20),
         name="hessian",

time: 63.7 us -> 62.2 us (0.976)
  Pallas kernels: 60.8 us -> 59.2 us
    pallas_call x1, Pallas kernels: 60.8 us -> 59.2 us  [shards(): pl.pallas_call(kernel, out_shape=(jax.ShapeDtypeStruct((MEMB, S, ROWS, LO...]
where the time goes in v8:
time: 62.2 us; the launch traced here: 62.1 us
  Pallas kernels  59.2 us (95%)
  local copies, waits for them, and re-layouts  2.22 us (4%)
  between operations  0.64 us (1%)
    pallas_call x1, Pallas kernels, shards(): pl.pallas_call(kernel, out_shape=(jax.ShapeDtypeStruct((MEMB, S, ROWS, LO...  59.2 us
    unnamed x2, local copies, waits for them, and re-layouts  2.22 us

profile of v8, /device:TPU:1, one launch (start us, length us, event | category | flops | bytes accessed | tf_op | source)
XLA Modules:
  0.0 62.1 jit_solution(9106012453913779023)
XLA Ops:
  0.6 59.2 %hessian.1 = (f32[2,4,80,720]{3,2,1,0:T(8,128)S(1)}, f32[4,80,720]{2,1,0:T(8,128)S(1)}) custom-call(bf16[2,4,80,720]{3,2,1,0:T(8,128)(2,1)} %alpha_hbm.1, bf16[4,80,720]{2,1,0:T(8,128)(2,1)} %static_hbm.1, bf16[2,180,4,320]{3,2,1,0:T(4,128)(2,1)} %bitcast.6, f32[180,4,320]{2,1,0:T(4,128)} %bitcast.7, bf16[720,720]{1,0:T(8,128)(2,1)} %lon_hbm.1, ...), custom_call_target="tpu_custom_call" | custom-call | tf_op jit(solution)/shard_map/hessian/pallas_call | solution.py:492
  59.9 1.3 %copy.15 = f32[2,4,80,720]{3,2,1,0:T(8,128)} copy(f32[2,4,80,720]{3,2,1,0:T(8,128)S(1)} %get-tuple-element.4) | data formatting | bytes 3686400
  61.2 0.9 %copy.16 = f32[4,80,720]{2,1,0:T(8,128)} copy(f32[4,80,720]{2,1,0:T(8,128)S(1)} %get-tuple-element.5) | data formatting | bytes 1843200

commit v9 on v8

--- a/solution.py
+++ b/solution.py
@@ -102,13 +102,12 @@
               (error_hbm, error_row), (weight_hbm, weight_row)]
     loads = [pltpu.make_async_copy(src, dst, load_sem.at[i]) for i, (src, dst) in enumerate(staged)]
     loads += [pltpu.make_async_copy(std_hbm.at[:, s, :], std.at[s], std_sem.at[s]) for s in range(S)]
-    for load in loads:
-        load.start()
-
     barrier = pltpu.get_barrier_semaphore()
     partners = to_t + to_y + [at_band(far), at_band(cross), at_band(sib)]
     for device in partners:
         pl.semaphore_signal(barrier, inc=1, device_id=device, device_id_type=MESH)
+    for load in loads:
+        load.start()
 
     def remote(src, dst, send, recv, device):
         return pltpu.make_async_remote_copy(

time: 62.2 us -> 62.7 us (level)
  no operation moved by 1% of the time
where the time goes in v9:
time: 62.7 us; the launch traced here: 62.6 us
  Pallas kernels  59.7 us (95%)
  local copies, waits for them, and re-layouts  2.22 us (4%)
  between operations  0.64 us (1%)
    pallas_call x1, Pallas kernels, shards(): pl.pallas_call(kernel, out_shape=(jax.ShapeDtypeStruct((MEMB, S, ROWS, LO...  59.7 us
    unnamed x2, local copies, waits for them, and re-layouts  2.22 us

profile of v9, /device:TPU:1, one launch (start us, length us, event | category | flops | bytes accessed | tf_op | source)
XLA Modules:
  0.0 62.6 jit_solution(17885301225457021915)
XLA Ops:
  0.6 59.7 %hessian.1 = (f32[2,4,80,720]{3,2,1,0:T(8,128)S(1)}, f32[4,80,720]{2,1,0:T(8,128)S(1)}) custom-call(bf16[2,4,80,720]{3,2,1,0:T(8,128)(2,1)} %alpha_hbm.1, bf16[4,80,720]{2,1,0:T(8,128)(2,1)} %static_hbm.1, bf16[2,180,4,320]{3,2,1,0:T(4,128)(2,1)} %bitcast.6, f32[180,4,320]{2,1,0:T(4,128)} %bitcast.7, bf16[720,720]{1,0:T(8,128)(2,1)} %lon_hbm.1, ...), custom_call_target="tpu_custom_call" | custom-call | tf_op jit(solution)/shard_map/hessian/pallas_call | solution.py:491
  60.4 1.3 %copy.15 = f32[2,4,80,720]{3,2,1,0:T(8,128)} copy(f32[2,4,80,720]{3,2,1,0:T(8,128)S(1)} %get-tuple-element.4) | data formatting | bytes 3686400
  61.6 0.9 %copy.16 = f32[4,80,720]{2,1,0:T(8,128)} copy(f32[4,80,720]{2,1,0:T(8,128)S(1)} %get-tuple-element.5) | data formatting | bytes 1843200
